TPU v7x, 32 devices: a whole 2x2x4 slice. The times are simulated.
32 devices in a mesh: freq: 8 (over y, x, core), rcv: 4 (over z).
Axes of the slice: x: 2, y: 2, z: 4, core: 2. Of those that a mesh axis runs over, the one named last changes fastest.
Arguments:
- green_freq: float32 [2, 8, 2304, 2304], P(None, 'freq', 'rcv'), may hold values from -6 to 6
- data_matrix: float32 [2, 8, 2304, 2304], P(None, 'freq', 'rcv'), may hold values from -0.09375 to 0.09375
- shot_panels: float32 [2, 8, 2304, 256], P(None, 'freq', 'rcv'), may hold values from -6 to 6
- wavelet: float32 [2, 8], P(None, 'freq'), may hold values from -1.5 to 1.5
- sources: int32 [256], replicated, may hold values from 0 to 2303, as said below
- support: int32 [8, 2304], replicated, may hold values 0 or 1
- threshold: float32 [1], replicated, may hold values from 3 to 7
Outputs:
- green_next: float32 [2, 8, 2304, 2304], P(None, 'freq', 'rcv')
- residual: float32 [2, 8, 2304, 256], P(None, 'freq', 'rcv')
Inputs may be any that keep to these rules, and one draw needn't show every extreme that they name: `sources`: 256 distinct source positions. `support`: a 0/1 mask over time samples and source positions.
All inputs are finite; a program needn't handle non-finite values.
Results may differ from a plain program's by a relative error of at most 0.00013.
Values sent between devices are 32-bit elements; how exact they have to be, the bound alone decides.
A program may use at most 128 MiB of HBM per device.

v0:
```python
import functools
import math

import jax
import jax.numpy as jnp
from jax import lax
from jax.experimental import pallas as pl
from jax.experimental.pallas import tpu as pltpu
from jax.sharding import PartitionSpec as P

HIGH = lax.Precision.HIGH
MESH = pl.DeviceIdType.MESH


def transform(points, sign):
    count = len(points)
    if count == 1:
        return points
    if count % 2:
        out = []
        for t in range(count):
            real, imag = points[0]
            for f in range(1, count):
                angle = sign * 2.0 * math.pi * (f * t % count) / count
                c, s = math.cos(angle), math.sin(angle)
                real = real + (c * points[f][0] - s * points[f][1])
                imag = imag + (s * points[f][0] + c * points[f][1])
            out.append((real, imag))
        return out
    even = transform(points[0::2], sign)
    odd = transform(points[1::2], sign)
    low, high = [], []
    for k in range(count // 2):
        er, ei = even[k]
        r, i = odd[k]
        angle = 8 * k / count
        if k == 0:
            tr, ti = r, i
        elif angle == 2:
            tr, ti = (-i, r) if sign > 0 else (i, -r)
        elif angle == 1:
            h = math.sqrt(0.5)
            tr, ti = (h * (r - i), h * (r + i)) if sign > 0 else (h * (r + i), h * (i - r))
        elif angle == 3:
            h = math.sqrt(0.5)
            tr, ti = (-h * (r + i), h * (r - i)) if sign > 0 else (h * (i - r), -h * (r + i))
        else:
            c = math.cos(2 * math.pi * k / count)
            s = sign * math.sin(2 * math.pi * k / count)
            tr, ti = c * r - s * i, s * r + c * i
        low.append((er + tr, ei + ti))
        high.append((er - tr, ei - ti))
    return low + high


def shrink_points(points, keep, level):
    count = len(points)
    timed = transform(points, 1)
    kept = []
    for t, (real, imag) in enumerate(timed):
        size = jnp.sqrt(real * real + imag * imag)
        factor = jnp.maximum(size - level, 0.0) / jnp.maximum(size, level) * keep[t : t + 1]
        factor = factor * (1.0 / count)
        kept.append((factor * real, factor * imag))
    return transform(kept, -1)


def shrink_body(scal_ref, keep_ref, *refs):
    *x_refs, o_ref = refs
    x_ref = x_refs[0]
    count = x_ref.shape[1]
    level = scal_ref[0]

    def lanes(j, carry):
        at = pl.ds(pl.multiple_of(j * 128, 128), 128)
        points = [(x_ref[0, f, :, at], x_ref[1, f, :, at]) for f in range(count)]
        if len(x_refs) == 2:
            d_ref = x_refs[1]
            step = scal_ref[1]
            points = [
                (r + step * d_ref[0, f, :, at], i + step * d_ref[1, f, :, at])
                for f, (r, i) in enumerate(points)
            ]
        out = shrink_points(points, keep_ref[:, at], level)
        for f in range(count):
            o_ref[0, f, :, at] = out[f][0]
            o_ref[1, f, :, at] = out[f][1]
        return carry

    lax.fori_loop(0, x_ref.shape[3] // 128, lanes, 0)


def shrink_call(scalars, keep, arrays):
    two, count, rows, width = arrays[0].shape
    tile = 8 if rows % 8 == 0 else rows
    if rows % 24 == 0 and width <= 512:
        tile = 24
    block = pl.BlockSpec((two, count, tile, width), lambda j: (0, 0, j, 0))
    size = arrays[0].size * 4
    return pl.pallas_call(
        shrink_body,
        grid=(rows // tile,),
        in_specs=[
            pl.BlockSpec(memory_space=pltpu.SMEM),
            pl.BlockSpec((count, width), lambda j: (0, 0)),
        ]
        + [block] * len(arrays),
        out_specs=block,
        out_shape=jax.ShapeDtypeStruct(arrays[0].shape, jnp.float32),
        cost_estimate=pl.CostEstimate(
            flops=40 * arrays[0].size, bytes_accessed=size * (1 + len(arrays)), transcendentals=0
        ),
    )(scalars, keep, *arrays)


def merge_body(mask_ref, hot_ref, cols_ref, back_ref, o_ref):
    hot = hot_ref[...]
    mask = mask_ref[...] > 0.5
    for part in range(2):
        x = cols_ref[:, part * hot.shape[0] : (part + 1) * hot.shape[0]]
        hi = x.astype(jnp.bfloat16)
        rest = x - hi.astype(jnp.float32)
        mid = rest.astype(jnp.bfloat16)
        low = (rest - mid.astype(jnp.float32)).astype(jnp.bfloat16)
        spread = (
            jnp.dot(hi, hot, preferred_element_type=jnp.float32)
            + jnp.dot(mid, hot, preferred_element_type=jnp.float32)
        ) + jnp.dot(low, hot, preferred_element_type=jnp.float32)
        o_ref[part, 0] = jnp.where(mask, spread, back_ref[part, 0])


def merge_call(mask, hot, cols, back):
    two, one, rows, width = back.shape
    picked = hot.shape[0]
    tile = rows // 4 if rows % 32 == 0 else rows
    return pl.pallas_call(
        merge_body,
        grid=(rows // tile,),
        in_specs=[
            pl.BlockSpec((1, width), lambda i: (0, 0)),
            pl.BlockSpec((picked, width), lambda i: (0, 0)),
            pl.BlockSpec((tile, two * picked), lambda i: (i, 0)),
            pl.BlockSpec((two, one, tile, width), lambda i: (0, 0, i, 0)),
        ],
        out_specs=pl.BlockSpec((two, one, tile, width), lambda i: (0, 0, i, 0)),
        out_shape=jax.ShapeDtypeStruct(back.shape, jnp.float32),
    )(mask, hot, cols, back)


def dots(lhs, rhs, contract):
    return lax.dot_general(lhs, rhs, (contract, ((), ())), precision=HIGH)


def apply_rows(data_real, data_imag, both, flipped):
    ahead = (((1,), (0,)))
    return dots(data_real, both, ahead) + dots(data_imag, flipped, ahead)


def ring_place(z, size):
    return jnp.where(z % 2 == 0, z // 2, size - 1 - z // 2)


def ring_owner(place, size):
    return jnp.where(2 * place < size, 2 * place, 2 * (size - 1 - place) + 1)


def ring_neighbours(size):
    z = lax.axis_index("rcv")
    place = ring_place(z, size)
    after = ring_owner((place + 1) % size, size)
    before = ring_owner((place + size - 1) % size, size)
    return z, place, after, before


def greet(freqs, after=None, before=None):
    me = lax.axis_index("freq")
    barrier = pltpu.get_barrier_semaphore()
    waits = freqs - 1
    for k in range(1, freqs):
        pl.semaphore_signal(
            barrier, inc=1, device_id={"freq": (me + k) % freqs}, device_id_type=MESH
        )
    if after is not None:
        for other in (after, before):
            pl.semaphore_signal(barrier, inc=1, device_id={"rcv": other}, device_id_type=MESH)
        waits += 2
    pl.semaphore_wait(barrier, waits)


def start_split(freqs, src, dst, sends, recvs, own):
    me = lax.axis_index("freq")
    rows = dst.shape[2]

    def part(j):
        return src.at[:, 0, pl.ds(pl.multiple_of(j * rows, 8), rows), :]

    copies = []
    for k in range(1, freqs):
        to = (me + k) % freqs
        copies.append(
            pltpu.make_async_remote_copy(
                part(to), dst.at[:, me], sends.at[k], recvs.at[k],
                device_id={"freq": to}, device_id_type=MESH,
            )
        )
    copies.append(pltpu.make_async_copy(part(me), dst.at[:, me], own))
    for copy in copies:
        copy.start()
    return copies


def start_join(freqs, src, dst, sends, recvs, own):
    me = lax.axis_index("freq")
    rows = src.shape[2]
    land = dst.at[:, 0, pl.ds(pl.multiple_of(me * rows, 8), rows), :]
    copies = []
    for k in range(1, freqs):
        to = (me + k) % freqs
        copies.append(
            pltpu.make_async_remote_copy(
                src.at[:, to], land, sends.at[k], recvs.at[k],
                device_id={"freq": to}, device_id_type=MESH,
            )
        )
    copies.append(pltpu.make_async_copy(src.at[:, me], land, own))
    for copy in copies:
        copy.start()
    return copies


def start_rows(freqs, src, dst, sends, recvs, own):
    me = lax.axis_index("freq")
    rows = dst.shape[1]

    def part(j):
        return src.at[pl.ds(pl.multiple_of(j * rows, 8), rows), :]

    copies = []
    for k in range(1, freqs):
        to = (me + k) % freqs
        copies.append(
            pltpu.make_async_remote_copy(
                part(to), dst.at[me], sends.at[k], recvs.at[k],
                device_id={"freq": to}, device_id_type=MESH,
            )
        )
    copies.append(pltpu.make_async_copy(part(me), dst.at[me], own))
    for copy in copies:
        copy.start()
    return copies


def ring_gather(size, place, after, blocks, sends, recvs):
    rows = blocks.shape[0] // size
    for step in range(size - 1):
        at = ring_owner((place + size - step) % size, size)
        part = blocks.at[pl.ds(pl.multiple_of(at * rows, 8), rows), :]
        copy = pltpu.make_async_remote_copy(
            part, part, sends.at[step], recvs.at[step],
            device_id={"rcv": after}, device_id_type=MESH,
        )
        copy.start()
        copy.wait()


def halves(x):
    hi = x.astype(jnp.bfloat16)
    return hi, (x - hi.astype(jnp.float32)).astype(jnp.bfloat16)


def product(lhs, rhs, contract):
    lh, ll = lhs
    rh, rl = rhs

    def dot(x, y):
        return lax.dot_general(x, y, (contract, ((), ())), preferred_element_type=jnp.float32)

    return (dot(lh, rl) + dot(ll, rh)) + dot(lh, rh)


CHUNK = 256


def apply_data(data, x_ref, acc):
    picks = x_ref.shape[1] // 2
    acc[...] = jnp.zeros_like(acc)

    def chunk(i, carry):
        at = pl.ds(pl.multiple_of(i * CHUNK, CHUNK), CHUNK)
        x = x_ref[at, :]
        turned = jnp.concatenate([-x[:, picks:], x[:, :picks]], axis=1)
        acc[...] += product(halves(data[0, :, at]), halves(x), ((1,), (0,)))
        acc[...] += product(halves(data[1, :, at]), halves(turned), ((1,), (0,)))
        return carry

    lax.fori_loop(0, x_ref.shape[0] // CHUNK, chunk, 0)


def apply_adjoint(data, x_ref, out):
    picks = x_ref.shape[1] // 2
    x = x_ref[...]
    straight = halves(x)
    turned = halves(jnp.concatenate([x[:, picks:], -x[:, :picks]], axis=1))

    def chunk(i, carry):
        at = pl.ds(pl.multiple_of(i * CHUNK, CHUNK), CHUNK)
        out[at, :] = product(halves(data[0, :, at]), straight, ((0,), (0,))) + product(
            halves(data[1, :, at]), turned, ((0,), (0,))
        )
        return carry

    lax.fori_loop(0, out.shape[0] // CHUNK, chunk, 0)


def first_body(
    freqs, size, level, wave, green, picked, shots, keep, data_hbm,
    gathered, shrunk, back, residual, norms, dir_timed, pick_timed,
    whole, dir_all, adjoint, local, held, total, data, image,
    fsend, frecv, fown, sends, recvs, own, arsend, arrecv, rsend, rrecv, gsend, grecv,
    dsend, drecv, down, psend, precv, pown, load,
):
    z, place, after, before = ring_neighbours(size)
    rows, both = picked.shape
    picks = both // 2

    def part(at):
        return pl.ds(pl.multiple_of(at * rows, 8), rows)

    fetch = pltpu.make_async_copy(data_hbm.at[:, 0], data, load)
    fetch.start()
    whole[part(z), :] = picked[...]
    greet(freqs, after, before)
    there = start_split(freqs, green, gathered, fsend, frecv, fown)
    ring_gather(size, place, after, whole, arsend, arrecv)
    fetch.wait()
    apply_data(data, whole, residual)
    wr, wi = wave[0], wave[1]
    re, im = slice(0, picks), slice(picks, both)
    rr = shots[:, re] - (wr * picked[:, re] - wi * picked[:, im] - residual[:, re])
    ri = shots[:, im] - (wr * picked[:, im] + wi * picked[:, re] - residual[:, im])
    residual[:, re] = rr
    residual[:, im] = ri
    local[:, re] = wr * rr + wi * ri
    local[:, im] = wr * ri - wi * rr
    apply_adjoint(data, residual, adjoint)
    copies = []
    for step in range(size - 1):
        at = ring_owner((place + 2 * size - 1 - step) % size, size)
        if step:
            total[step - 1] = held[step - 1] + adjoint[part(at), :]
        copy = pltpu.make_async_remote_copy(
            adjoint.at[part(at), :] if step == 0 else total.at[step - 1],
            held.at[step], rsend.at[step], rrecv.at[step],
            device_id={"rcv": after}, device_id_type=MESH,
        )
        copy.start()
        if step == 0:
            for sent in there:
                sent.wait()
            two, count, deep, width = gathered.shape
            block = pl.BlockSpec((two, count, 8, width), lambda j: (0, 0, j, 0))
            pltpu.emit_pipeline(
                lambda x, o: shrink_body(level, keep, x, o),
                grid=(deep // 8,),
                in_specs=[block],
                out_specs=[block],
            )(gathered, shrunk)
            copies += start_join(freqs, shrunk, back, sends, recvs, own)
            copies += start_rows(freqs, picked, pick_timed, psend, precv, pown)
        copy.wait()
    dir_all[part(z), :] = local[...] - (held[size - 2] + adjoint[part(z), :])
    copies += start_rows(freqs, dir_all.at[part(z), :], dir_timed, dsend, drecv, down)
    ring_gather(size, place, after, dir_all, gsend, grecv)
    apply_data(data, dir_all, image)
    mine = dir_all[part(z), :]
    gr = wr * mine[:, re] - wi * mine[:, im] - image[:, re]
    gi = wr * mine[:, im] + wi * mine[:, re] - image[:, im]
    norms[0] = jnp.full((8, 128), jnp.sum(mine * mine))
    norms[1] = jnp.full((8, 128), jnp.sum(gr * gr + gi * gi))
    for copy in copies:
        copy.wait()


def third_body(
    freqs, size, level_ref, norms, keep, picks, dirs, out,
    freq_box, rcv_box, cols, fsend, frecv, zsend, zrecv, sends, recvs, own,
):
    me = lax.axis_index("freq")
    z = lax.axis_index("rcv")
    barrier = pltpu.get_barrier_semaphore()
    for k in range(1, freqs):
        pl.semaphore_signal(
            barrier, inc=1, device_id={"freq": (me + k) % freqs}, device_id_type=MESH
        )
    for k in range(1, size):
        pl.semaphore_signal(barrier, inc=1, device_id={"rcv": (z + k) % size}, device_id_type=MESH)
    pl.semaphore_wait(barrier, freqs + size - 2)

    copies = []
    for k in range(1, freqs):
        copies.append(
            pltpu.make_async_remote_copy(
                norms, freq_box.at[k], fsend.at[k], frecv.at[k],
                device_id={"freq": (me + k) % freqs}, device_id_type=MESH,
            )
        )
    for copy in copies:
        copy.start()
    for copy in copies:
        copy.wait()
    parts = norms[...]
    for k in range(1, freqs):
        parts = parts + freq_box[k]
    rcv_box[0] = parts
    copies = []
    for k in range(1, size):
        copies.append(
            pltpu.make_async_remote_copy(
                rcv_box.at[0], rcv_box.at[k], zsend.at[k], zrecv.at[k],
                device_id={"rcv": (z + k) % size}, device_id_type=MESH,
            )
        )
    for copy in copies:
        copy.start()
    for copy in copies:
        copy.wait()
    total = rcv_box[0]
    for k in range(1, size):
        total = total + rcv_box[k]
    step = total[0] / total[1]
    level = level_ref[0]
    count = picks.shape[2] // 2

    def tile(i, carry):
        rows = pl.ds(pl.multiple_of(i * 8, 8), 8)
        for lane in range(0, count, 128):
            re = slice(lane, lane + 128)
            im = slice(count + lane, count + lane + 128)
            points = [
                (
                    picks[f, rows, re] + step * dirs[f, rows, re],
                    picks[f, rows, im] + step * dirs[f, rows, im],
                )
                for f in range(freqs)
            ]
            done = shrink_points(points, keep[:, re], level)
            for f in range(freqs):
                cols[f, rows, re] = done[f][0]
                cols[f, rows, im] = done[f][1]
        return carry

    lax.fori_loop(0, picks.shape[1] // 8, tile, 0)
    rows = cols.shape[1]
    land = out.at[pl.ds(pl.multiple_of(me * rows, 8), rows), :]
    copies = []
    for k in range(1, freqs):
        to = (me + k) % freqs
        copies.append(
            pltpu.make_async_remote_copy(
                cols.at[to], land, sends.at[k], recvs.at[k],
                device_id={"freq": to}, device_id_type=MESH,
            )
        )
    copies.append(pltpu.make_async_copy(cols.at[me], land, own))
    for copy in copies:
        copy.start()
    for copy in copies:
        copy.wait()


ANY = pl.BlockSpec(memory_space=pltpu.HBM)
VMEM = pl.BlockSpec(memory_space=pltpu.VMEM)
DMA = pltpu.SemaphoreType.DMA


SMEM = pl.BlockSpec(memory_space=pltpu.SMEM)


def first_call(freqs, size, level, wave, green, picked, shots, keep, data):
    two, _, rows, width = green.shape
    both = picked.shape[1]
    deep = rows // freqs
    f32 = jnp.float32
    split = jax.ShapeDtypeStruct((two, freqs, deep, width), f32)
    timed = jax.ShapeDtypeStruct((freqs, deep, both), f32)
    tall = pltpu.VMEM((size * rows, both), f32)
    flat = pltpu.VMEM((rows, both), f32)
    trio = [DMA((freqs,)), DMA((freqs,)), DMA(())]
    ring = [DMA((size,)), DMA((size,))]
    return pl.pallas_call(
        functools.partial(first_body, freqs, size),
        out_shape=(
            split,
            split,
            jax.ShapeDtypeStruct(green.shape, f32),
            jax.ShapeDtypeStruct(picked.shape, f32),
            jax.ShapeDtypeStruct((2, 8, 128), f32),
            timed,
            timed,
        ),
        in_specs=[SMEM, SMEM, ANY, VMEM, VMEM, VMEM, ANY],
        out_specs=(ANY, ANY, ANY, VMEM, VMEM, VMEM, VMEM),
        scratch_shapes=[
            tall, tall, tall, flat,
            pltpu.VMEM((size - 1, rows, both), f32),
            pltpu.VMEM((size - 2, rows, both), f32),
            pltpu.VMEM((two, rows, width), f32),
            flat,
        ]
        + trio + trio + ring + ring + ring + trio + trio + [DMA(())],
        compiler_params=pltpu.CompilerParams(
            collective_id=0, has_side_effects=True, vmem_limit_bytes=60 << 20
        ),
    )(level, wave, green, picked, shots, keep, data)


def third_call(freqs, size, level, norms, keep, picks, dirs):
    _, part, both = picks.shape
    return pl.pallas_call(
        functools.partial(third_body, freqs, size),
        out_shape=jax.ShapeDtypeStruct((part * freqs, both), jnp.float32),
        in_specs=[pl.BlockSpec(memory_space=pltpu.SMEM), VMEM, VMEM, VMEM, VMEM],
        out_specs=VMEM,
        scratch_shapes=[
            pltpu.VMEM((freqs, 2, 8, 128), jnp.float32),
            pltpu.VMEM((size, 2, 8, 128), jnp.float32),
            pltpu.VMEM((freqs, part, both), jnp.float32),
            DMA((freqs,)), DMA((freqs,)), DMA((size,)), DMA((size,)),
            DMA((freqs,)), DMA((freqs,)), DMA(()),
        ],
        compiler_params=pltpu.CompilerParams(
            collective_id=2, has_side_effects=True, vmem_limit_bytes=32 << 20
        ),
    )(level, norms, keep, picks, dirs)


def pick_body(hot_ref, x_ref, o_ref):
    picks = hot_ref.shape[1]
    hot = hot_ref[...]
    for part in range(2):
        x = x_ref[part, 0]
        hi = x.astype(jnp.bfloat16)
        rest = x - hi.astype(jnp.float32)
        mid = rest.astype(jnp.bfloat16)
        low = (rest - mid.astype(jnp.float32)).astype(jnp.bfloat16)
        o_ref[:, part * picks : (part + 1) * picks] = (
            jnp.dot(hi, hot, preferred_element_type=jnp.float32)
            + jnp.dot(mid, hot, preferred_element_type=jnp.float32)
        ) + jnp.dot(low, hot, preferred_element_type=jnp.float32)


def pick_call(hot, green):
    two, one, rows, width = green.shape
    picks = hot.shape[1]
    tile = rows // 4 if rows % 32 == 0 else rows
    return pl.pallas_call(
        pick_body,
        grid=(rows // tile,),
        in_specs=[
            pl.BlockSpec((width, picks), lambda i: (0, 0)),
            pl.BlockSpec((two, one, tile, width), lambda i: (0, 0, i, 0)),
        ],
        out_specs=pl.BlockSpec((tile, 2 * picks), lambda i: (i, 0)),
        out_shape=jax.ShapeDtypeStruct((rows, 2 * picks), jnp.float32),
    )(hot, green)


def on_device(green_freq, data_matrix, shot_panels, wavelet, sources, support, threshold):
    width = green_freq.shape[3]
    rows_here = green_freq.shape[2]
    picks = sources.shape[0]
    keep_all = support.astype(jnp.float32)
    freqs = lax.axis_size("freq")
    size = lax.axis_size("rcv")
    fast = rows_here % (8 * freqs) == 0 and size % 2 == 0 and size > 2
    fast = fast and width % CHUNK == 0 and picks % 128 == 0
    places = jnp.arange(width, dtype=jnp.int32)
    pickcat = pick_call((places[:, None] == sources[None, :]).astype(jnp.bfloat16), green_freq)
    picked = (pickcat[:, :picks], pickcat[:, picks:])
    keep_cols = jnp.take(keep_all, sources, axis=1)
    wr = wavelet[0, 0]
    wi = wavelet[1, 0]
    if fast:
        wave = wavelet[:, 0]
        shots = jnp.concatenate([shot_panels[0, 0], shot_panels[1, 0]], axis=1)
        _, _, back, resid, norms, dir_timed, pick_timed = first_call(
            freqs, size, threshold, wave, green_freq, pickcat, shots, keep_all, data_matrix
        )
        cols_back = third_call(
            freqs, size, threshold, norms, keep_cols, pick_timed, dir_timed
        )
        residual = jnp.stack([resid[:, :picks], resid[:, picks:]])[:, None]
    else:
        gathered = lax.all_to_all(green_freq, "freq", split_axis=2, concat_axis=1, tiled=True)
        both = lax.all_gather(pickcat, "rcv", axis=0, tiled=True)
        dr = data_matrix[0, 0]
        di = data_matrix[1, 0]
        flipped = jnp.concatenate([-both[:, picks:], both[:, :picks]], axis=1)
        multiple = apply_rows(dr, di, both, flipped)
        resid_real = shot_panels[0, 0] - (wr * picked[0] - wi * picked[1] - multiple[:, :picks])
        resid_imag = shot_panels[1, 0] - (wr * picked[1] + wi * picked[0] - multiple[:, picks:])
        residual = jnp.stack([resid_real, resid_imag])[:, None]
        down = ((0,), (0,))
        rboth = jnp.concatenate([resid_real, resid_imag], axis=1)
        rflip = jnp.concatenate([resid_imag, -resid_real], axis=1)
        adjoint = dots(dr, rboth, down) + dots(di, rflip, down)
        local = jnp.concatenate(
            [wr * resid_real + wi * resid_imag, wr * resid_imag - wi * resid_real], axis=1
        )
        direction = local - lax.psum_scatter(adjoint, "rcv", scatter_dimension=0, tiled=True)
        dir_all = lax.all_gather(direction, "rcv", axis=0, tiled=True)
        shrunk = shrink_call(threshold, keep_all, (gathered,))
        back = lax.all_to_all(shrunk, "freq", split_axis=1, concat_axis=2, tiled=True)
        dir_real = direction[:, :picks]
        dir_imag = direction[:, picks:]
        dir_timed = lax.all_to_all(
            jnp.stack([dir_real, dir_imag])[:, None],
            "freq", split_axis=2, concat_axis=1, tiled=True,
        )
        pushed = apply_rows(
            dr, di, dir_all, jnp.concatenate([-dir_all[:, picks:], dir_all[:, :picks]], axis=1)
        )
        image_real = wr * dir_real - wi * dir_imag - pushed[:, :picks]
        image_imag = wr * dir_imag + wi * dir_real - pushed[:, picks:]
        norm_dir = jnp.sum(direction * direction)
        norm_img = jnp.sum(image_real * image_real + image_imag * image_imag)
        totals = lax.psum(jnp.stack([norm_dir, norm_img]), ("freq", "rcv"))
        scalars = jnp.concatenate([threshold, (totals[0] / totals[1])[None]])
        pick_timed = jnp.take(gathered, sources, axis=3)
        cols = shrink_call(scalars, keep_cols, (pick_timed, dir_timed))
        cols_back = lax.all_to_all(cols, "freq", split_axis=1, concat_axis=2, tiled=True)
        cols_back = jnp.concatenate([cols_back[0, 0], cols_back[1, 0]], axis=1)
    hot = sources[:, None] == places[None, :]
    mask = jnp.any(hot, axis=0, keepdims=True).astype(jnp.float32)
    green_next = merge_call(mask, hot.astype(jnp.bfloat16), cols_back, back)
    return (green_next, residual)


def solution(mesh):
    in_specs = (
        P(None, "freq", "rcv", None),
        P(None, "freq", "rcv", None),
        P(None, "freq", "rcv", None),
        P(None, "freq"),
        P(),
        P(),
        P(),
    )
    out_specs = (P(None, "freq", "rcv", None), P(None, "freq", "rcv", None))
    return jax.shard_map(
        on_device, mesh=mesh, in_specs=in_specs, out_specs=out_specs, check_vma=False
    )
```

profile of v0, /device:TPU:1, one launch (start us, length us, event | category | flops | bytes accessed | tf_op | source)
XLA Modules:
  0.0 341.0 jit_solution(8188738674360991573)
XLA Ops:
  0.6 1.3 slice_bitcast_fusion.3
  2.0 0.0 copy-start.6
  2.0 0.0 copy-start.7
  2.0 1.2 pad_maximum_fusion.shots
  3.2 0.0 copy-done.6
  3.2 0.6 convert_element_type.18.keep
  4.5 0.0 copy-done.7
  4.5 1.6 fusion.2.hot_ref
  6.1 8.5 %shard_map.86.picked = f32[576,512]{1,0:T(8,128)} custom-call(bf16[2304,256]{1,0:T(8,128)(2,1)} %fusion.2.hot_ref, f32[2,1,576,2304]{3,2,1,0:T(8,128)} %green.1), custom_call_target="tpu_custom_call" | custom-call | tf_op jit(solution)/shard_map/pallas_call | solution.py:556
  14.5 0.0 copy-start.5
  14.5 277.9 %shard_map.87 = (f32[2,8,72,2304]{3,2,1,0:T(8,128)}, f32[2,8,72,2304]{3,2,1,0:T(8,128)}, f32[2,1,576,2304]{3,2,1,0:T(8,128)}, f32[576,512]{1,0:T(8,128)}, f32[2,...) custom-call(f32[1]{0:T(128)S(6)} %copy.12.level.level_ref, f32[2]{0:T(128)} %bitcast.15, ...), custom_call_target="tpu_custom_call" | custom-call | tf_op jit(solution)/shard_map/pallas_call | solution.py:490
  292.4 0.0 copy-start.1
  292.4 0.0 copy-start.3
  292.4 0.0 copy-done.5
  292.4 0.4 copy.9
  292.8 0.7 gather_fusion
  293.6 0.1 copy.10
  293.6 0.0 copy-done.1
  293.7 0.0 copy-done.3
  293.7 0.0 copy-start.2
  293.7 1.3 copy-done.2
  294.9 30.3 %shard_map.88.cols_ref = f32[576,512]{1,0:T(8,128)S(1)} custom-call(f32[1]{0:T(128)S(6)} %copy.12.level.level_ref, f32[2,8,128]{2,1,0:T(8,128)S(1)} %copy-done.3, f32[8,256]{1,0:T(8,128)S(1)} %select_bitcast_fusion.keep, f32[8,72,512]{2,1,0:T(8,128)S(1)} %copy-done.2, f32[8,72,512]{2,1,0:T(8,128)S(1)} %copy-done.1), custom_call_target="tpu_custom_call" | custom-call | tf_op jit(solution)/shard_map/pallas_call | solution.py:519
  325.3 0.0 copy-start
  325.3 1.0 copy-done
  326.3 1.6 fusion
  328.0 0.6 reshape.21.mask_ref
  328.6 0.0 copy-start.4
  328.6 11.2 %shard_map.89 = f32[2,1,576,2304]{3,2,1,0:T(8,128)} custom-call(f32[1,2304]{1,0:T(1,128)} %reshape.21.mask_ref, bf16[256,2304]{1,0:T(8,128)(2,1)} %get-tuple-element.18.hot_ref, f32[576,512]{1,0:T(8,128)} %copy-done, f32[2,1,576,2304]{3,2,1,0:T(8,128)} %get-tuple-element.10.back_ref), custom_call_target="tpu_custom_call" | custom-call | tf_op jit(solution)/shard_map/pallas_call | solution.py:136
  339.8 0.0 copy-done.4
  339.8 0.1 slice_bitcast_fusion.1
  339.9 1.1 maximum_bitcast_fusion
  (5 shorter events, 0.0 us)
Async XLA Ops:
  2.0 1.2 copy-start.6
  2.0 2.5 copy-start.7
  14.5 277.9 %copy-start.5 = (f32[8,2304]{1,0:T(8,128)S(1)}, f32[8,2304]{1,0:T(8,128)}, u32[]{:S(2)}) copy-start(f32[8,2304]{1,0:T(8,128)} %convert_element_type.18.keep) | copy-start | bytes 221188
  292.4 1.3 copy-start.1
  292.4 1.3 copy-start.3
  293.7 1.3 copy-start.2
  325.3 1.0 copy-start
  328.6 11.2 %copy-start.4 = (f32[576,512]{1,0:T(8,128)S(1)}, f32[576,512]{1,0:T(8,128)}, u32[]{:S(2)}) copy-start(f32[576,512]{1,0:T(8,128)} %get-tuple-element.11) | copy-start | bytes 3538948
where the time goes:
time: 342 us; the launch traced here: 341 us
  Pallas kernels  328 us (96%)
  other arithmetic  6.21 us (2%)
  local copies, waits for them, and re-layouts  5.52 us (2%)
    pallas_call x1, Pallas kernels, first_call(): pl.pallas_call(functools.partial(first_body, freqs, size), out_shape=(spl...  278 us
    pallas_call x1, Pallas kernels, third_call(): pl.pallas_call(functools.partial(third_body, freqs, size), out_shape=jax....  30.3 us
    pallas_call x1, Pallas kernels, merge_call(): pl.pallas_call(merge_body, grid=(rows // tile,), in_specs=[pl.BlockSpec((...  11.2 us
    pallas_call x1, Pallas kernels, pick_call(): pl.pallas_call(pick_body, grid=(rows // tile,), in_specs=[pl.BlockSpec((w...  8.46 us

commit v1 on v0

v1 whole, which is shorter than its diff:
```python
import functools
import math

import jax
import jax.numpy as jnp
from jax import lax
from jax.experimental import pallas as pl
from jax.experimental.pallas import tpu as pltpu
from jax.sharding import PartitionSpec as P

HIGH = lax.Precision.HIGH
MESH = pl.DeviceIdType.MESH


def transform(points, sign):
    count = len(points)
    if count == 1:
        return points
    if count % 2:
        out = []
        for t in range(count):
            real, imag = points[0]
            for f in range(1, count):
                angle = sign * 2.0 * math.pi * (f * t % count) / count
                c, s = math.cos(angle), math.sin(angle)
                real = real + (c * points[f][0] - s * points[f][1])
                imag = imag + (s * points[f][0] + c * points[f][1])
            out.append((real, imag))
        return out
    even = transform(points[0::2], sign)
    odd = transform(points[1::2], sign)
    low, high = [], []
    for k in range(count // 2):
        er, ei = even[k]
        r, i = odd[k]
        angle = 8 * k / count
        if k == 0:
            tr, ti = r, i
        elif angle == 2:
            tr, ti = (-i, r) if sign > 0 else (i, -r)
        elif angle == 1:
            h = math.sqrt(0.5)
            tr, ti = (h * (r - i), h * (r + i)) if sign > 0 else (h * (r + i), h * (i - r))
        elif angle == 3:
            h = math.sqrt(0.5)
            tr, ti = (-h * (r + i), h * (r - i)) if sign > 0 else (h * (i - r), -h * (r + i))
        else:
            c = math.cos(2 * math.pi * k / count)
            s = sign * math.sin(2 * math.pi * k / count)
            tr, ti = c * r - s * i, s * r + c * i
        low.append((er + tr, ei + ti))
        high.append((er - tr, ei - ti))
    return low + high


def shrink_points(points, keep, level):
    count = len(points)
    timed = transform(points, 1)
    kept = []
    for t, (real, imag) in enumerate(timed):
        size = jnp.sqrt(real * real + imag * imag)
        factor = jnp.maximum(size - level, 0.0) / jnp.maximum(size, level) * keep[t : t + 1]
        factor = factor * (1.0 / count)
        kept.append((factor * real, factor * imag))
    return transform(kept, -1)


def shrink_body(scal_ref, keep_ref, *refs):
    *x_refs, o_ref = refs
    x_ref = x_refs[0]
    count = x_ref.shape[1]
    level = scal_ref[0]

    def lanes(j, carry):
        at = pl.ds(pl.multiple_of(j * 128, 128), 128)
        points = [(x_ref[0, f, :, at], x_ref[1, f, :, at]) for f in range(count)]
        if len(x_refs) == 2:
            d_ref = x_refs[1]
            step = scal_ref[1]
            points = [
                (r + step * d_ref[0, f, :, at], i + step * d_ref[1, f, :, at])
                for f, (r, i) in enumerate(points)
            ]
        out = shrink_points(points, keep_ref[:, at], level)
        for f in range(count):
            o_ref[0, f, :, at] = out[f][0]
            o_ref[1, f, :, at] = out[f][1]
        return carry

    lax.fori_loop(0, x_ref.shape[3] // 128, lanes, 0)


def shrink_call(scalars, keep, arrays):
    two, count, rows, width = arrays[0].shape
    tile = 8 if rows % 8 == 0 else rows
    if rows % 24 == 0 and width <= 512:
        tile = 24
    block = pl.BlockSpec((two, count, tile, width), lambda j: (0, 0, j, 0))
    size = arrays[0].size * 4
    return pl.pallas_call(
        shrink_body,
        grid=(rows // tile,),
        in_specs=[
            pl.BlockSpec(memory_space=pltpu.SMEM),
            pl.BlockSpec((count, width), lambda j: (0, 0)),
        ]
        + [block] * len(arrays),
        out_specs=block,
        out_shape=jax.ShapeDtypeStruct(arrays[0].shape, jnp.float32),
        cost_estimate=pl.CostEstimate(
            flops=40 * arrays[0].size, bytes_accessed=size * (1 + len(arrays)), transcendentals=0
        ),
    )(scalars, keep, *arrays)


def merge_body(mask_ref, hot_ref, cols_ref, back_ref, o_ref):
    hot = hot_ref[...]
    mask = mask_ref[...] > 0.5
    for part in range(2):
        x = cols_ref[:, part * hot.shape[0] : (part + 1) * hot.shape[0]]
        hi = x.astype(jnp.bfloat16)
        rest = x - hi.astype(jnp.float32)
        mid = rest.astype(jnp.bfloat16)
        low = (rest - mid.astype(jnp.float32)).astype(jnp.bfloat16)
        spread = (
            jnp.dot(hi, hot, preferred_element_type=jnp.float32)
            + jnp.dot(mid, hot, preferred_element_type=jnp.float32)
        ) + jnp.dot(low, hot, preferred_element_type=jnp.float32)
        o_ref[part, 0] = jnp.where(mask, spread, back_ref[part, 0])


def merge_call(mask, hot, cols, back):
    two, one, rows, width = back.shape
    picked = hot.shape[0]
    tile = rows // 4 if rows % 32 == 0 else rows
    return pl.pallas_call(
        merge_body,
        grid=(rows // tile,),
        in_specs=[
            pl.BlockSpec((1, width), lambda i: (0, 0)),
            pl.BlockSpec((picked, width), lambda i: (0, 0)),
            pl.BlockSpec((tile, two * picked), lambda i: (i, 0)),
            pl.BlockSpec((two, one, tile, width), lambda i: (0, 0, i, 0)),
        ],
        out_specs=pl.BlockSpec((two, one, tile, width), lambda i: (0, 0, i, 0)),
        out_shape=jax.ShapeDtypeStruct(back.shape, jnp.float32),
    )(mask, hot, cols, back)


def dots(lhs, rhs, contract):
    return lax.dot_general(lhs, rhs, (contract, ((), ())), precision=HIGH)


def apply_rows(data_real, data_imag, both, flipped):
    ahead = (((1,), (0,)))
    return dots(data_real, both, ahead) + dots(data_imag, flipped, ahead)


ANY = pl.BlockSpec(memory_space=pltpu.HBM)
VMEM = pl.BlockSpec(memory_space=pltpu.VMEM)
DMA = pltpu.SemaphoreType.DMA


SMEM = pl.BlockSpec(memory_space=pltpu.SMEM)


def halves(x):
    hi = x.astype(jnp.bfloat16)
    return hi, (x - hi.astype(jnp.float32)).astype(jnp.bfloat16)


def thirds(x):
    hi, mid = halves(x)
    rest = x - hi.astype(jnp.float32) - mid.astype(jnp.float32)
    return jnp.concatenate([hi, mid, rest.astype(jnp.bfloat16)], axis=0)


def select(x, hot):
    rows = x.shape[0]
    out = jnp.dot(thirds(x), hot, preferred_element_type=jnp.float32)
    return (out[:rows] + out[rows : 2 * rows]) + out[2 * rows :]


def six(parts, contract):
    total = None
    for (lh, ll), (rh, rl) in parts:
        for x, y in ((lh, rl), (ll, rh), (lh, rh)):
            term = lax.dot_general(
                x, y, (contract, ((), ())), preferred_element_type=jnp.float32
            )
            total = term if total is None else total + term
    return total


def piece_of(width):
    for piece in (768, 512, 256):
        if width % piece == 0:
            return piece
    return width


def apply_data(data, x_ref, acc):
    half = x_ref.shape[1] // 2
    piece = piece_of(x_ref.shape[0])
    acc[...] = jnp.zeros_like(acc)

    def chunk(i, carry):
        at = pl.ds(pl.multiple_of(i * piece, piece), piece)
        x = x_ref[at, :]
        turned = jnp.concatenate([-x[:, half:], x[:, :half]], axis=1)
        acc[...] += six(
            [
                ((data[0, 0, :, at], data[0, 1, :, at]), halves(x)),
                ((data[1, 0, :, at], data[1, 1, :, at]), halves(turned)),
            ],
            ((1,), (0,)),
        )
        return carry

    lax.fori_loop(0, x_ref.shape[0] // piece, chunk, 0)


def apply_adjoint(data, x, out):
    half = x.shape[1] // 2
    piece = piece_of(out.shape[0])
    straight = halves(x)
    turned = halves(jnp.concatenate([x[:, half:], -x[:, :half]], axis=1))

    def chunk(i, carry):
        at = pl.ds(pl.multiple_of(i * piece, piece), piece)
        out[at, :] = six(
            [
                ((data[0, 0, :, at], data[0, 1, :, at]), straight),
                ((data[1, 0, :, at], data[1, 1, :, at]), turned),
            ],
            ((0,), (0,)),
        )
        return carry

    lax.fori_loop(0, out.shape[0] // piece, chunk, 0)


class Gather:
    def __init__(self, size, buf, sends, recvs):
        self.size, self.buf, self.sends, self.recvs = size, buf, sends, recvs
        self.z = lax.axis_index("rcv")

    def ways(self, step):
        z, last = self.z, self.size - 1
        rows = self.buf.shape[0] // self.size
        for way in range(2):
            if way == 0:
                block, to = jnp.maximum(z - step, 0), jnp.minimum(z + 1, last)
                sent = (z < last) & (z >= step)
                got = z >= step + 1
            else:
                block, to = jnp.minimum(z + step, last), jnp.maximum(z - 1, 0)
                sent = (z > 0) & (z + step <= last)
                got = z + 1 + step <= last
            part = self.buf.at[pl.ds(pl.multiple_of(block * rows, 8), rows), :]
            copy = pltpu.make_async_remote_copy(
                part, part, self.sends.at[way, step], self.recvs.at[way, step],
                device_id={"rcv": to}, device_id_type=MESH,
            )
            yield copy, sent, got

    def start(self, step):
        for copy, sent, _ in self.ways(step):
            pl.when(sent)(copy.start)

    def recv(self, step):
        for copy, _, got in self.ways(step):
            pl.when(got)(copy.wait_recv)

    def drain(self):
        for step in range(self.size - 1):
            for copy, sent, _ in self.ways(step):
                pl.when(sent)(copy.wait_send)


class Scatter:
    def __init__(self, size, terms, held, sends, recvs):
        self.size, self.terms, self.held = size, terms, held
        self.sends, self.recvs = sends, recvs
        self.z = lax.axis_index("rcv")

    def ways(self, step):
        z, last = self.z, self.size - 1
        rows = self.terms.shape[0] // self.size
        for way in range(2):
            if way == 0:
                far, to = z, jnp.minimum(z + 1, last)
                block = jnp.minimum(last - step + z, last)
                more, less = z < last, z > 0
            else:
                far, to = last - z, jnp.maximum(z - 1, 0)
                block = jnp.maximum(step - last + z, 0)
                more, less = z > 0, z < last
            own = self.terms.at[pl.ds(pl.multiple_of(block * rows, 8), rows), :]
            got = less & (step >= far - 1)
            yield way, own, to, more & (far == 0), more & (far > 0) & (step >= far), got

    def copy(self, src, way, step, to):
        return pltpu.make_async_remote_copy(
            src, self.held.at[way, step], self.sends.at[way, step], self.recvs.at[way, step],
            device_id={"rcv": to}, device_id_type=MESH,
        )

    def start(self, step):
        for way, own, to, first, later, _ in self.ways(step):
            pl.when(first)(self.copy(own, way, step, to).start)
            if step:
                self.pass_on(way, own, to, step, later)

    def pass_on(self, way, own, to, step, later):
        @pl.when(later)
        def _():
            self.held[way, step - 1] = self.held[way, step - 1] + own[...]
            self.copy(self.held.at[way, step - 1], way, step, to).start()

    def recv(self, step):
        for way, own, to, _, _, got in self.ways(step):
            pl.when(got)(self.copy(own, way, step, to).wait_recv)

    def drain(self):
        for step in range(self.size - 1):
            for way, own, to, first, later, _ in self.ways(step):
                pl.when(first | later)(self.copy(own, way, step, to).wait_send)


def greet(freqs, size):
    me = lax.axis_index("freq")
    z = lax.axis_index("rcv")
    barrier = pltpu.get_barrier_semaphore()
    for k in range(1, freqs):
        pl.semaphore_signal(
            barrier, inc=1, device_id={"freq": (me + k) % freqs}, device_id_type=MESH
        )
    for k in range(1, size):
        pl.semaphore_signal(barrier, inc=1, device_id={"rcv": (z + k) % size}, device_id_type=MESH)
    pl.semaphore_wait(barrier, freqs + size - 2)


LINE = 8


def rows_at(at, count):
    return pl.ds(pl.multiple_of(at, 8), count)


def main_body(
    freqs, size, level_ref, wave, srcs, support, green, data_hbm, shots_hbm,
    gathered, shrunk, back, cols_out, residual, hot_out, mask_out,
    big, data, whole, dir_all, adjoint, held, local, shots, image, hot, keep, keep_cols,
    pick_timed, dir_timed, cols, norms, freq_box, rcv_box,
    gload, sload, load, fsend, frecv, fown, bsend, brecv, bown,
    zsend, zrecv, dsend, drecv, down, csend, crecv, cown, nfs, nfr, nzs, nzr,
):
    me = lax.axis_index("freq")
    z = lax.axis_index("rcv")
    _, _, rows, width = green.shape
    deep = rows // freqs
    lines = deep // LINE
    picks = srcs.shape[1]
    half = picks // 2
    mine = rows_at(z * rows, rows)
    parts = gload.shape[0]
    tall = rows // parts

    def loading(j):
        at = rows_at(j * tall, tall)
        return pltpu.make_async_copy(green.at[:, 0, at, :], big.at[:, at, :], gload.at[j])

    for j in range(parts):
        loading(j).start()
    fetch_shots = pltpu.make_async_copy(shots_hbm.at[:, 0], shots, sload)
    fetch_shots.start()
    greet(freqs, size)

    def forth(i, k):
        to = (me + k) % freqs
        return pltpu.make_async_remote_copy(
            green.at[:, 0, rows_at(to * deep + i * LINE, LINE), :],
            gathered.at[:, me, pl.ds(i * LINE, LINE), :],
            fsend.at[i, k], frecv.at[i, k],
            device_id={"freq": to}, device_id_type=MESH,
        )

    for i in range(lines):
        for k in range(1, freqs):
            forth(i, k).start()

    place = lax.broadcasted_iota(jnp.int32, (width, picks), 0)
    hot_f32 = jnp.where(place == srcs[...], 1.0, 0.0)
    hot[...] = hot_f32.astype(jnp.bfloat16)

    def pick(j, carry):
        at = rows_at(j * tall, tall)
        loading(j).wait()
        for part in range(2):
            out = select(big[part, at, :], hot[...])
            to = rows_at(z * rows + j * tall, tall)
            for c in range(2):
                whole[c, to, part * half : (part + 1) * half] = out[:, c * half : (c + 1) * half]
        return carry

    lax.fori_loop(0, parts, pick, 0)
    first = [Gather(size, whole.at[c], zsend.at[c], zrecv.at[c]) for c in range(2)]
    second = [Gather(size, dir_all.at[c], zsend.at[2 + c], zrecv.at[2 + c]) for c in range(2)]
    sums = [
        Scatter(size, adjoint.at[c], held.at[c], zsend.at[4 + c], zrecv.at[4 + c])
        for c in range(2)
    ]
    last = size - 2
    first[0].start(0)
    own_part = pltpu.make_async_copy(
        big.at[:, rows_at(me * deep, deep), :], gathered.at[:, me], fown
    )
    own_part.start()
    keep[...] = support[...].astype(jnp.float32)
    keep_cols[...] = jnp.dot(
        keep[...].astype(jnp.bfloat16), hot[...], preferred_element_type=jnp.float32
    )
    for at in range(0, width, picks):
        hot_out[:, at : at + picks] = hot[at : at + picks, :].astype(jnp.float32).T.astype(
            jnp.bfloat16
        )
    mask_out[...] = jnp.dot(
        jnp.ones((8, picks), jnp.bfloat16), hot_out[...], preferred_element_type=jnp.float32
    )
    own_part.wait()
    fetch = pltpu.make_async_copy(data_hbm.at[:, 0], big, load)
    fetch.start()

    def split(j, carry):
        at = rows_at(j * 32, 32)
        for part in range(2):
            hi, lo = halves(big[part, at, :])
            data[part, 0, at, :] = hi
            data[part, 1, at, :] = lo
        return carry

    def shrink(lo, count):
        for i in range(lo, lo + count):
            for k in range(1, freqs):
                forth(i, k).wait_recv()
        block = pl.BlockSpec((2, freqs, LINE, width), lambda j: (0, 0, lo + j, 0))

        def body(ids, x_ref, o_ref):
            flat = x_ref[...].reshape(2 * freqs * LINE, width)
            got = select(flat, hot[...])
            at = rows_at((lo + ids.index[0]) * LINE, LINE)
            for part in range(2):
                for f in range(freqs):
                    row = (part * freqs + f) * LINE
                    pick_timed[f, at, part * picks : (part + 1) * picks] = got[row : row + LINE, :]
            shrink_body(level_ref, keep, x_ref, o_ref)

        pltpu.emit_pipeline(
            body, grid=(count,), in_specs=[block], out_specs=[block], _explicit_indices=True
        )(gathered, shrunk)

    def back_copy(i, k):
        to = (me + k) % freqs
        return pltpu.make_async_remote_copy(
            shrunk.at[:, to, pl.ds(i * LINE, LINE), :],
            back.at[:, 0, rows_at(me * deep + i * LINE, LINE), :],
            bsend.at[i, k], brecv.at[i, k],
            device_id={"freq": to}, device_id_type=MESH,
        )

    def back_own(i):
        return pltpu.make_async_copy(
            shrunk.at[:, me, pl.ds(i * LINE, LINE), :],
            back.at[:, 0, rows_at(me * deep + i * LINE, LINE), :],
            bown.at[i],
        )

    def give(lo, count):
        for i in range(lo, lo + count):
            for k in range(1, freqs):
                back_copy(i, k).start()
            back_own(i).start()

    def rows_copy(c, k):
        to = (me + k) % freqs
        return pltpu.make_async_remote_copy(
            dir_all.at[c, rows_at(z * rows + to * deep, deep), :], dir_timed.at[c, me],
            dsend.at[c, k], drecv.at[c, k],
            device_id={"freq": to}, device_id_type=MESH,
        )

    def rows_own(c):
        return pltpu.make_async_copy(
            dir_all.at[c, rows_at(z * rows + me * deep, deep), :], dir_timed.at[c, me], down.at[c]
        )

    wr, wi = wave[0], wave[1]
    re, im = slice(0, half), slice(half, 2 * half)

    def residual_of(c):
        apply_data(data, whole.at[c], image)
        at = slice(c * half, (c + 1) * half)
        pr, pi = whole[c, mine, re], whole[c, mine, im]
        rr = shots[0, :, at] - (wr * pr - wi * pi - image[:, re])
        ri = shots[1, :, at] - (wr * pi + wi * pr - image[:, im])
        residual[0, 0, :, at] = rr
        residual[1, 0, :, at] = ri
        local[c, :, re] = wr * rr + wi * ri
        local[c, :, im] = wr * ri - wi * rr
        apply_adjoint(data, jnp.concatenate([rr, ri], axis=1), adjoint.at[c])

    def direction_of(c):
        dir_all[c, mine, :] = local[c] - adjoint[c, mine, :]

        @pl.when(z > 0)
        def _():
            dir_all[c, mine, :] = dir_all[c, mine, :] - held[c, 0, last]

        @pl.when(z < size - 1)
        def _():
            dir_all[c, mine, :] = dir_all[c, mine, :] - held[c, 1, last]

    def send_direction(c):
        for k in range(1, freqs):
            rows_copy(c, k).start()
        rows_own(c).start()

    def image_of(c):
        apply_data(data, dir_all.at[c], image)
        dr, di = dir_all[c, mine, re], dir_all[c, mine, im]
        gr = wr * dr - wi * di - image[:, re]
        gi = wr * di + wi * dr - image[:, im]
        return jnp.sum(dr * dr + di * di), jnp.sum(gr * gr + gi * gi)

    first[0].recv(0)
    first[0].start(1)
    fetch.wait()
    lax.fori_loop(0, rows // 32, split, 0)
    fetch_shots.wait()
    first[0].recv(1)
    first[0].start(2)
    first[1].start(0)
    shrink(0, 2)
    first[0].recv(2)
    residual_of(0)
    sums[0].start(0)
    first[1].recv(0)
    first[1].start(1)
    shrink(2, 2)
    sums[0].recv(0)
    sums[0].start(1)
    first[1].recv(1)
    first[1].start(2)
    shrink(4, 1)
    sums[0].recv(1)
    sums[0].start(2)
    first[1].recv(2)
    residual_of(1)
    sums[1].start(0)
    sums[0].recv(2)
    direction_of(0)
    second[0].start(0)
    send_direction(0)
    shrink(5, 2)
    give(0, 2)
    sums[1].recv(0)
    sums[1].start(1)
    second[0].recv(0)
    second[0].start(1)
    shrink(7, 1)
    give(2, 1)
    sums[1].recv(1)
    sums[1].start(2)
    second[0].recv(1)
    second[0].start(2)
    shrink(8, lines - 8)
    give(3, 1)
    sums[1].recv(2)
    direction_of(1)
    second[1].start(0)
    send_direction(1)
    second[0].recv(2)
    ones = image_of(0)
    give(4, 1)
    second[1].recv(0)
    second[1].start(1)
    give(5, 1)
    second[1].recv(1)
    second[1].start(2)
    give(6, 1)
    second[1].recv(2)
    twos = image_of(1)

    for n in range(2):
        norms[n] = jnp.full((8, 128), ones[n] + twos[n])

    def spread(k):
        return pltpu.make_async_remote_copy(
            norms, freq_box.at[k], nfs.at[k], nfr.at[k],
            device_id={"freq": (me + k) % freqs}, device_id_type=MESH,
        )

    def across(k):
        return pltpu.make_async_remote_copy(
            rcv_box.at[0], rcv_box.at[k], nzs.at[k], nzr.at[k],
            device_id={"rcv": (z + k) % size}, device_id_type=MESH,
        )

    for k in range(1, freqs):
        spread(k).start()
    give(7, lines - 7)
    parts_sum = norms[...]
    for k in range(1, freqs):
        spread(k).wait_recv()
        parts_sum = parts_sum + freq_box[k]
    rcv_box[0] = parts_sum
    for k in range(1, size):
        across(k).start()
    total = parts_sum
    for k in range(1, size):
        across(k).wait_recv()
        total = total + rcv_box[k]
    step = total[0] / total[1]
    level = level_ref[0]
    for c in range(2):
        for k in range(1, freqs):
            rows_copy(c, k).wait_recv()
        rows_own(c).wait()

    def tile(i, carry):
        at = rows_at(i * 8, 8)
        for lane in range(0, picks, 128):
            c, off = lane // half, lane % half
            points = [
                (
                    pick_timed[f, at, lane : lane + 128]
                    + step * dir_timed[c, f, at, off : off + 128],
                    pick_timed[f, at, picks + lane : picks + lane + 128]
                    + step * dir_timed[c, f, at, half + off : half + off + 128],
                )
                for f in range(freqs)
            ]
            done = shrink_points(points, keep_cols[:, lane : lane + 128], level)
            for f in range(freqs):
                cols[f, at, lane : lane + 128] = done[f][0]
                cols[f, at, picks + lane : picks + lane + 128] = done[f][1]
        return carry

    lax.fori_loop(0, deep // 8, tile, 0)
    land = cols_out.at[rows_at(me * deep, deep), :]

    def cols_copy(k):
        to = (me + k) % freqs
        return pltpu.make_async_remote_copy(
            cols.at[to], land, csend.at[k], crecv.at[k],
            device_id={"freq": to}, device_id_type=MESH,
        )

    cols_own = pltpu.make_async_copy(cols.at[me], land, cown)
    for k in range(1, freqs):
        cols_copy(k).start()
    cols_own.start()
    for group in first + second + sums:
        group.drain()
    for i in range(lines):
        for k in range(1, freqs):
            forth(i, k).wait_send()
            back_copy(i, k).wait()
        back_own(i).wait()
    for k in range(1, freqs):
        spread(k).wait_send()
        for c in range(2):
            rows_copy(c, k).wait_send()
        cols_copy(k).wait()
    cols_own.wait()
    for k in range(1, size):
        across(k).wait_send()


def main_call(freqs, size, level, wave, srcs, support, green, data, shots):
    two, _, rows, width = green.shape
    picks = srcs.shape[1]
    deep = rows // freqs
    lines = deep // LINE
    f32, bf16 = jnp.float32, jnp.bfloat16
    split = jax.ShapeDtypeStruct((two, freqs, deep, width), f32)
    vmem = pltpu.VMEM
    return pl.pallas_call(
        functools.partial(main_body, freqs, size),
        out_shape=(
            split,
            split,
            jax.ShapeDtypeStruct(green.shape, f32),
            jax.ShapeDtypeStruct((rows, two * picks), f32),
            jax.ShapeDtypeStruct((two, 1, rows, picks), f32),
            jax.ShapeDtypeStruct((picks, width), bf16),
            jax.ShapeDtypeStruct((8, width), f32),
        ),
        in_specs=[SMEM, SMEM, VMEM, VMEM, ANY, ANY, ANY],
        out_specs=(ANY, ANY, ANY, ANY, VMEM, VMEM, VMEM),
        scratch_shapes=[
            vmem((two, rows, width), f32),
            vmem((two, 2, rows, width), bf16),
            vmem((2, size * rows, picks), f32),
            vmem((2, size * rows, picks), f32),
            vmem((2, size * rows, picks), f32),
            vmem((2, 2, size - 1, rows, picks), f32),
            vmem((2, rows, picks), f32),
            vmem((two, rows, picks), f32),
            vmem((rows, picks), f32),
            vmem((width, picks), bf16),
            vmem((8, width), f32),
            vmem((8, picks), f32),
            vmem((freqs, deep, two * picks), f32),
            vmem((2, freqs, deep, picks), f32),
            vmem((freqs, deep, two * picks), f32),
            vmem((2, 8, 128), f32),
            vmem((freqs, 2, 8, 128), f32),
            vmem((size, 2, 8, 128), f32),
            DMA((4,)), DMA(()), DMA(()),
            DMA((lines, freqs)), DMA((lines, freqs)), DMA(()),
            DMA((lines, freqs)), DMA((lines, freqs)), DMA((lines,)),
            DMA((6, 2, size)), DMA((6, 2, size)),
            DMA((2, freqs)), DMA((2, freqs)), DMA((2,)),
            DMA((freqs,)), DMA((freqs,)), DMA(()),
            DMA((freqs,)), DMA((freqs,)), DMA((size,)), DMA((size,)),
        ],
        compiler_params=pltpu.CompilerParams(
            collective_id=0, has_side_effects=True, vmem_limit_bytes=67043328
        ),
    )(level, wave, srcs, support, green, data, shots)


def join_body(mask_ref, hot_ref, cols_ref, back_ref, resid_ref, o_ref, r_ref):
    picks = hot_ref.shape[0]
    hot = hot_ref[...]
    mask = mask_ref[0:1, :] > 0.5
    for part in range(2):
        spread = select(cols_ref[:, part * picks : (part + 1) * picks], hot)
        o_ref[part, 0] = jnp.where(mask, spread, back_ref[part, 0])
    r_ref[...] = resid_ref[...]


def join_call(mask, hot, cols, back, resid):
    two, one, rows, width = back.shape
    picks = hot.shape[0]
    tile = rows // 8 if rows % 64 == 0 else rows
    wide = pl.BlockSpec((two, one, tile, width), lambda i: (0, 0, i, 0))
    thin = pl.BlockSpec((two, one, tile, picks), lambda i: (0, 0, i, 0))
    return pl.pallas_call(
        join_body,
        grid=(rows // tile,),
        in_specs=[
            pl.BlockSpec((8, width), lambda i: (0, 0)),
            pl.BlockSpec((picks, width), lambda i: (0, 0)),
            pl.BlockSpec((tile, two * picks), lambda i: (i, 0)),
            wide,
            thin,
        ],
        out_specs=[wide, thin],
        out_shape=[
            jax.ShapeDtypeStruct(back.shape, jnp.float32),
            jax.ShapeDtypeStruct(resid.shape, jnp.float32),
        ],
    )(mask, hot, cols, back, resid)


def pick_body(hot_ref, x_ref, o_ref):
    picks = hot_ref.shape[1]
    hot = hot_ref[...]
    for part in range(2):
        x = x_ref[part, 0]
        hi = x.astype(jnp.bfloat16)
        rest = x - hi.astype(jnp.float32)
        mid = rest.astype(jnp.bfloat16)
        low = (rest - mid.astype(jnp.float32)).astype(jnp.bfloat16)
        o_ref[:, part * picks : (part + 1) * picks] = (
            jnp.dot(hi, hot, preferred_element_type=jnp.float32)
            + jnp.dot(mid, hot, preferred_element_type=jnp.float32)
        ) + jnp.dot(low, hot, preferred_element_type=jnp.float32)


def pick_call(hot, green):
    two, one, rows, width = green.shape
    picks = hot.shape[1]
    tile = rows // 4 if rows % 32 == 0 else rows
    return pl.pallas_call(
        pick_body,
        grid=(rows // tile,),
        in_specs=[
            pl.BlockSpec((width, picks), lambda i: (0, 0)),
            pl.BlockSpec((two, one, tile, width), lambda i: (0, 0, i, 0)),
        ],
        out_specs=pl.BlockSpec((tile, 2 * picks), lambda i: (i, 0)),
        out_shape=jax.ShapeDtypeStruct((rows, 2 * picks), jnp.float32),
    )(hot, green)


def on_device(green_freq, data_matrix, shot_panels, wavelet, sources, support, threshold):
    width = green_freq.shape[3]
    rows_here = green_freq.shape[2]
    picks = sources.shape[0]
    freqs = lax.axis_size("freq")
    size = lax.axis_size("rcv")
    fast = rows_here % (LINE * freqs) == 0 and size > 2 and rows_here // freqs >= 8 * LINE
    fast = fast and rows_here % 32 == 0 and width % picks == 0 and picks % 256 == 0
    if fast:
        _, _, back, cols, resid, hot, mask = main_call(
            freqs, size, threshold, wavelet[:, 0], sources[None, :], support,
            green_freq, data_matrix, shot_panels,
        )
        green_next, residual = join_call(mask, hot, cols, back, resid)
        return (green_next, residual)
    keep_all = support.astype(jnp.float32)
    places = jnp.arange(width, dtype=jnp.int32)
    pickcat = pick_call((places[:, None] == sources[None, :]).astype(jnp.bfloat16), green_freq)
    picked = (pickcat[:, :picks], pickcat[:, picks:])
    keep_cols = jnp.take(keep_all, sources, axis=1)
    wr = wavelet[0, 0]
    wi = wavelet[1, 0]
    gathered = lax.all_to_all(green_freq, "freq", split_axis=2, concat_axis=1, tiled=True)
    both = lax.all_gather(pickcat, "rcv", axis=0, tiled=True)
    dr = data_matrix[0, 0]
    di = data_matrix[1, 0]
    flipped = jnp.concatenate([-both[:, picks:], both[:, :picks]], axis=1)
    multiple = apply_rows(dr, di, both, flipped)
    resid_real = shot_panels[0, 0] - (wr * picked[0] - wi * picked[1] - multiple[:, :picks])
    resid_imag = shot_panels[1, 0] - (wr * picked[1] + wi * picked[0] - multiple[:, picks:])
    residual = jnp.stack([resid_real, resid_imag])[:, None]
    down = ((0,), (0,))
    rboth = jnp.concatenate([resid_real, resid_imag], axis=1)
    rflip = jnp.concatenate([resid_imag, -resid_real], axis=1)
    adjoint = dots(dr, rboth, down) + dots(di, rflip, down)
    local = jnp.concatenate(
        [wr * resid_real + wi * resid_imag, wr * resid_imag - wi * resid_real], axis=1
    )
    direction = local - lax.psum_scatter(adjoint, "rcv", scatter_dimension=0, tiled=True)
    dir_all = lax.all_gather(direction, "rcv", axis=0, tiled=True)
    shrunk = shrink_call(threshold, keep_all, (gathered,))
    back = lax.all_to_all(shrunk, "freq", split_axis=1, concat_axis=2, tiled=True)
    dir_real = direction[:, :picks]
    dir_imag = direction[:, picks:]
    dir_timed = lax.all_to_all(
        jnp.stack([dir_real, dir_imag])[:, None],
        "freq", split_axis=2, concat_axis=1, tiled=True,
    )
    pushed = apply_rows(
        dr, di, dir_all, jnp.concatenate([-dir_all[:, picks:], dir_all[:, :picks]], axis=1)
    )
    image_real = wr * dir_real - wi * dir_imag - pushed[:, :picks]
    image_imag = wr * dir_imag + wi * dir_real - pushed[:, picks:]
    norm_dir = jnp.sum(direction * direction)
    norm_img = jnp.sum(image_real * image_real + image_imag * image_imag)
    totals = lax.psum(jnp.stack([norm_dir, norm_img]), ("freq", "rcv"))
    scalars = jnp.concatenate([threshold, (totals[0] / totals[1])[None]])
    pick_timed = jnp.take(gathered, sources, axis=3)
    cols = shrink_call(scalars, keep_cols, (pick_timed, dir_timed))
    cols_back = lax.all_to_all(cols, "freq", split_axis=1, concat_axis=2, tiled=True)
    cols_back = jnp.concatenate([cols_back[0, 0], cols_back[1, 0]], axis=1)
    hot = sources[:, None] == places[None, :]
    mask = jnp.any(hot, axis=0, keepdims=True).astype(jnp.float32)
    green_next = merge_call(mask, hot.astype(jnp.bfloat16), cols_back, back)
    return (green_next, residual)


def solution(mesh):
    in_specs = (
        P(None, "freq", "rcv", None),
        P(None, "freq", "rcv", None),
        P(None, "freq", "rcv", None),
        P(None, "freq"),
        P(),
        P(),
        P(),
    )
    out_specs = (P(None, "freq", "rcv", None), P(None, "freq", "rcv", None))
    return jax.shard_map(
        on_device, mesh=mesh, in_specs=in_specs, out_specs=out_specs, check_vma=False
    )
```

time: 342 us -> 284 us (0.83)
  Pallas kernels: 328 us -> 282 us
  other arithmetic: 6.21 us -> 0 us
  local copies, waits for them, and re-layouts: 5.52 us -> 0 us
    pallas_call x4 -> x2, Pallas kernels: 328 us -> 282 us  [the longest x1 268 us: main_call(): pl.pallas_call(functools.partial(main_body, freqs, size), out_shape=(spli...]
    convert_element_type x4 -> x0, other arithmetic: 3.87 us -> none  [the longest x1 1.65 us: on_device(): green_next = merge_call(mask, hot.astype(jnp.bfloat16), cols_back, back)]
where the time goes in v1:
time: 284 us; the launch traced here: 283 us
  Pallas kernels  282 us (99%)
    pallas_call x1, Pallas kernels, main_call(): pl.pallas_call(functools.partial(main_body, freqs, size), out_shape=(spli...  268 us
    pallas_call x1, Pallas kernels, join_call(): pl.pallas_call(join_body, grid=(rows // tile,), in_specs=[pl.BlockSpec((8...  14 us

profile of v1, /device:TPU:1, one launch (start us, length us, event | category | flops | bytes accessed | tf_op | source)
XLA Modules:
  0.0 283.0 jit_solution(10637160270812609230)
XLA Ops:
  1.3 267.7 %shard_map.86 = (f32[2,8,72,2304]{3,2,1,0:T(8,128)}, f32[2,8,72,2304]{3,2,1,0:T(8,128)}, f32[2,1,576,2304]{3,2,1,0:T(8,128)}, f32[576,512]{1,0:T(8,128)}, f32[2,...) custom-call(f32[1]{0:T(128)S(6)} %copy.9.level_ref, f32[2]{0:T(128)} %bitcast.3, ...), custom_call_target="tpu_custom_call" | custom-call | tf_op jit(solution)/shard_map/pallas_call | solution.py:689
  269.0 14.0 %shard_map.87 = (f32[2,1,576,2304]{3,2,1,0:T(8,128)}, f32[2,1,576,256]{3,2,1,0:T(8,128)}) custom-call(f32[8,2304]{1,0:T(8,128)} %get-tuple-element.7.mask_ref, bf16[256,2304]{1,0:T(8,128)(2,1)} %get-tuple-element.8.hot_ref, f32[576,512]{1,0:T(8,128)} %get-tuple-element.9.cols_ref, f32[2,1,576,2304]{3,2,1,0:T(8,128)} %get-tuple-element.10.back_ref, ...), custom_call_target="tpu_custom_call" | custom-call | tf_op jit(solution)/shard_map/pallas_call | solution.py:751

commit v2 on v1

--- a/solution.py
+++ b/solution.py
@@ -181,6 +181,15 @@
     return (out[:rows] + out[rows : 2 * rows]) + out[2 * rows :]
 
 
+def spread(x, hot):
+    hi, mid = halves(x)
+    low = (x - hi.astype(jnp.float32) - mid.astype(jnp.float32)).astype(jnp.bfloat16)
+    return (
+        jnp.dot(hi, hot, preferred_element_type=jnp.float32)
+        + jnp.dot(mid, hot, preferred_element_type=jnp.float32)
+    ) + jnp.dot(low, hot, preferred_element_type=jnp.float32)
+
+
 def six(parts, contract):
     total = None
     for (lh, ll), (rh, rl) in parts:
@@ -350,9 +359,9 @@
 
 def main_body(
     freqs, size, level_ref, wave, srcs, support, green, data_hbm, shots_hbm,
-    gathered, shrunk, back, cols_out, residual, hot_out, mask_out,
-    big, data, whole, dir_all, adjoint, held, local, shots, image, hot, keep, keep_cols,
-    pick_timed, dir_timed, cols, norms, freq_box, rcv_box,
+    gathered, shrunk, back, tails, cols_out, residual, hot_out, mask_out,
+    big, data, whole, dir_all, adjoint, held, local, shots, image, hot, fill, lead,
+    keep, keep_cols, timed, cols, norms, freq_box, rcv_box,
     gload, sload, load, fsend, frecv, fown, bsend, brecv, bown,
     zsend, zrecv, dsend, drecv, down, csend, crecv, cown, nfs, nfr, nzs, nzr,
 ):
@@ -363,6 +372,7 @@
     lines = deep // LINE
     picks = srcs.shape[1]
     half = picks // 2
+    head = width - picks
     mine = rows_at(z * rows, rows)
     parts = gload.shape[0]
     tall = rows // parts
@@ -375,28 +385,97 @@
         loading(j).start()
     fetch_shots = pltpu.make_async_copy(shots_hbm.at[:, 0], shots, sload)
     fetch_shots.start()
-    greet(freqs, size)
+    slots = [box.at[c, rows_at(n * rows, rows), :]
+             for box in (adjoint, dir_all) for c in range(2) for n in range(size)]
+    slots += [held.at[c, way, n] for c in range(2) for way in range(2) for n in range(size - 1)]
+    places = [(part, at) for part in range(2) for at in range(0, width, picks)]
+    slots = slots[: len(places)]
+
+    def fetching(n):
+        part, at = places[n]
+        return pltpu.make_async_copy(
+            data_hbm.at[part, 0, :, pl.ds(at, picks)], slots[n], load.at[n]
+        )
+
+    for n in range(len(places)):
+        fetching(n).start()
+
+    def packed(i, to):
+        if isinstance(i, int) and i == 0:
+            return lead.at[:, rows_at(to * LINE, LINE), :]
+        return big.at[:, rows_at(to * deep + i * LINE, LINE), pl.ds(0, head)]
 
     def forth(i, k):
         to = (me + k) % freqs
         return pltpu.make_async_remote_copy(
-            green.at[:, 0, rows_at(to * deep + i * LINE, LINE), :],
-            gathered.at[:, me, pl.ds(i * LINE, LINE), :],
+            packed(i, to), gathered.at[:, me, rows_at(i * LINE, LINE), :],
             fsend.at[i, k], frecv.at[i, k],
             device_id={"freq": to}, device_id_type=MESH,
         )
 
-    for i in range(lines):
+    def forth_own(i):
+        return pltpu.make_async_copy(
+            packed(i, me), gathered.at[:, me, rows_at(i * LINE, LINE), :], fown.at[i]
+        )
+
+    def send_forth(i):
         for k in range(1, freqs):
             forth(i, k).start()
+        forth_own(i).start()
 
     place = lax.broadcasted_iota(jnp.int32, (width, picks), 0)
-    hot_f32 = jnp.where(place == srcs[...], 1.0, 0.0)
-    hot[...] = hot_f32.astype(jnp.bfloat16)
+    hot[...] = jnp.where(place == srcs[...], 1.0, 0.0).astype(jnp.bfloat16)
+    before = jnp.where(srcs[...] < place, 1.0, 0.0)
+    ones = jnp.ones((8, picks), jnp.bfloat16)
+    across_lanes = (((1,), (1,)), ((), ()))
+    mask_out[...] = lax.dot_general(
+        ones, hot[...], across_lanes, preferred_element_type=jnp.float32
+    )
+    rank = lax.dot_general(
+        ones, before.astype(jnp.bfloat16), across_lanes, preferred_element_type=jnp.float32
+    )
+    ends = jnp.sum(before[head:, :], axis=1, keepdims=True)
+    spare = 1.0 - jnp.sum(
+        hot[head:, :].astype(jnp.float32), axis=1, keepdims=True
+    )
+    order = lax.broadcasted_iota(jnp.int32, (picks, 1), 0).astype(jnp.float32)
+    order = order - (ends - ends[0:1, :])
+    taken = mask_out[0:1, :head] > 0.5
+    fill[...] = jnp.where(
+        taken & (spare > 0.5) & (rank[0:1, :head] == order), 1.0, 0.0
+    ).astype(jnp.bfloat16)
+
+    def pack(x):
+        got = spread(x[:, head:], fill[...])
+        return jnp.where(mask_out[0:1, :head] > 0.5, got, x[:, :head])
+
+    def line_of(i):
+        return jnp.concatenate(
+            [big[part, rows_at(o * deep + i * LINE, LINE), :] for part in range(2)
+             for o in range(freqs)], axis=0,
+        )
+
+    for j in range(parts):
+        loading(j).wait()
+    lead_rows = pack(line_of(0))
+    for part in range(2):
+        lead[part] = lead_rows[part * freqs * LINE : (part + 1) * freqs * LINE]
+    keep_all = support[...].astype(jnp.float32)
+    keep[...] = jnp.where(
+        taken,
+        jnp.dot(
+            keep_all[:, head:].astype(jnp.bfloat16), fill[...], preferred_element_type=jnp.float32
+        ),
+        keep_all[:, :head],
+    )
+    keep_cols[...] = jnp.dot(
+        keep_all.astype(jnp.bfloat16), hot[...], preferred_element_type=jnp.float32
+    )
+    greet(freqs, size)
+    send_forth(0)
 
     def pick(j, carry):
         at = rows_at(j * tall, tall)
-        loading(j).wait()
         for part in range(2):
             out = select(big[part, at, :], hot[...])
             to = rows_at(z * rows + j * tall, tall)
@@ -405,6 +484,14 @@
         return carry
 
     lax.fori_loop(0, parts, pick, 0)
+    for n, (part, at) in enumerate(places):
+        fetching(n).wait()
+        for row in range(0, rows, rows // 2):
+            there = slice(row, row + rows // 2)
+            hi, lo = halves(slots[n][there, :])
+            data[part, 0, there, at : at + picks] = hi
+            data[part, 1, there, at : at + picks] = lo
+
     first = [Gather(size, whole.at[c], zsend.at[c], zrecv.at[c]) for c in range(2)]
     second = [Gather(size, dir_all.at[c], zsend.at[2 + c], zrecv.at[2 + c]) for c in range(2)]
     sums = [
@@ -413,51 +500,31 @@
     ]
     last = size - 2
     first[0].start(0)
-    own_part = pltpu.make_async_copy(
-        big.at[:, rows_at(me * deep, deep), :], gathered.at[:, me], fown
-    )
-    own_part.start()
-    keep[...] = support[...].astype(jnp.float32)
-    keep_cols[...] = jnp.dot(
-        keep[...].astype(jnp.bfloat16), hot[...], preferred_element_type=jnp.float32
-    )
+    def pack_line(i, carry):
+        done = pack(line_of(i))
+        for part in range(2):
+            for o in range(freqs):
+                row = (part * freqs + o) * LINE
+                big[part, rows_at(o * deep + i * LINE, LINE), 0:head] = done[row : row + LINE]
+        return carry
+
+    lax.fori_loop(1, lines, pack_line, 0)
+    for i in range(1, lines):
+        send_forth(i)
     for at in range(0, width, picks):
         hot_out[:, at : at + picks] = hot[at : at + picks, :].astype(jnp.float32).T.astype(
             jnp.bfloat16
         )
-    mask_out[...] = jnp.dot(
-        jnp.ones((8, picks), jnp.bfloat16), hot_out[...], preferred_element_type=jnp.float32
-    )
-    own_part.wait()
-    fetch = pltpu.make_async_copy(data_hbm.at[:, 0], big, load)
-    fetch.start()
-
-    def split(j, carry):
-        at = rows_at(j * 32, 32)
-        for part in range(2):
-            hi, lo = halves(big[part, at, :])
-            data[part, 0, at, :] = hi
-            data[part, 1, at, :] = lo
-        return carry
 
     def shrink(lo, count):
         for i in range(lo, lo + count):
             for k in range(1, freqs):
                 forth(i, k).wait_recv()
-        block = pl.BlockSpec((2, freqs, LINE, width), lambda j: (0, 0, lo + j, 0))
-
-        def body(ids, x_ref, o_ref):
-            flat = x_ref[...].reshape(2 * freqs * LINE, width)
-            got = select(flat, hot[...])
-            at = rows_at((lo + ids.index[0]) * LINE, LINE)
-            for part in range(2):
-                for f in range(freqs):
-                    row = (part * freqs + f) * LINE
-                    pick_timed[f, at, part * picks : (part + 1) * picks] = got[row : row + LINE, :]
-            shrink_body(level_ref, keep, x_ref, o_ref)
-
+            forth_own(i).wait()
+        block = pl.BlockSpec((2, freqs, LINE, head), lambda j: (0, 0, lo + j, 0))
         pltpu.emit_pipeline(
-            body, grid=(count,), in_specs=[block], out_specs=[block], _explicit_indices=True
+            lambda x, o: shrink_body(level_ref, keep, x, o),
+            grid=(count,), in_specs=[block], out_specs=[block],
         )(gathered, shrunk)
 
     def back_copy(i, k):
@@ -485,14 +552,14 @@
     def rows_copy(c, k):
         to = (me + k) % freqs
         return pltpu.make_async_remote_copy(
-            dir_all.at[c, rows_at(z * rows + to * deep, deep), :], dir_timed.at[c, me],
+            local.at[c, rows_at(to * deep, deep), :], timed.at[c, me],
             dsend.at[c, k], drecv.at[c, k],
             device_id={"freq": to}, device_id_type=MESH,
         )
 
     def rows_own(c):
         return pltpu.make_async_copy(
-            dir_all.at[c, rows_at(z * rows + me * deep, deep), :], dir_timed.at[c, me], down.at[c]
+            local.at[c, rows_at(me * deep, deep), :], timed.at[c, me], down.at[c]
         )
 
     wr, wi = wave[0], wave[1]
@@ -521,7 +588,8 @@
         def _():
             dir_all[c, mine, :] = dir_all[c, mine, :] - held[c, 1, last]
 
-    def send_direction(c):
+    def send_update(c, step):
+        local[c] = whole[c, mine, :] + step * dir_all[c, mine, :]
         for k in range(1, freqs):
             rows_copy(c, k).start()
         rows_own(c).start()
@@ -535,8 +603,6 @@
 
     first[0].recv(0)
     first[0].start(1)
-    fetch.wait()
-    lax.fori_loop(0, rows // 32, split, 0)
     fetch_shots.wait()
     first[0].recv(1)
     first[0].start(2)
@@ -561,41 +627,39 @@
     sums[0].recv(2)
     direction_of(0)
     second[0].start(0)
-    send_direction(0)
     shrink(5, 2)
-    give(0, 2)
+    give(0, 3)
     sums[1].recv(0)
     sums[1].start(1)
     second[0].recv(0)
     second[0].start(1)
     shrink(7, 1)
-    give(2, 1)
+    give(3, 1)
     sums[1].recv(1)
     sums[1].start(2)
     second[0].recv(1)
     second[0].start(2)
     shrink(8, lines - 8)
-    give(3, 1)
+    give(4, 1)
     sums[1].recv(2)
     direction_of(1)
     second[1].start(0)
-    send_direction(1)
     second[0].recv(2)
-    ones = image_of(0)
-    give(4, 1)
+    first_norms = image_of(0)
+    give(5, 1)
     second[1].recv(0)
     second[1].start(1)
-    give(5, 1)
+    give(6, 1)
     second[1].recv(1)
     second[1].start(2)
-    give(6, 1)
+    give(7, lines - 7)
     second[1].recv(2)
-    twos = image_of(1)
+    second_norms = image_of(1)
 
     for n in range(2):
-        norms[n] = jnp.full((8, 128), ones[n] + twos[n])
-
-    def spread(k):
+        norms[n] = jnp.full((8, 128), first_norms[n] + second_norms[n])
+
+    def along(k):
         return pltpu.make_async_remote_copy(
             norms, freq_box.at[k], nfs.at[k], nfr.at[k],
             device_id={"freq": (me + k) % freqs}, device_id_type=MESH,
@@ -608,11 +672,10 @@
         )
 
     for k in range(1, freqs):
-        spread(k).start()
-    give(7, lines - 7)
+        along(k).start()
     parts_sum = norms[...]
     for k in range(1, freqs):
-        spread(k).wait_recv()
+        along(k).wait_recv()
         parts_sum = parts_sum + freq_box[k]
     rcv_box[0] = parts_sum
     for k in range(1, size):
@@ -624,56 +687,78 @@
     step = total[0] / total[1]
     level = level_ref[0]
     for c in range(2):
+        send_update(c, step[0:1, 0:1])
+
+    def cols_copy(c, k):
+        to = (me + k) % freqs
+        return pltpu.make_async_remote_copy(
+            cols.at[c, to], cols_out.at[rows_at(me * deep, deep), pl.ds(c * picks, picks)],
+            csend.at[c, k], crecv.at[c, k],
+            device_id={"freq": to}, device_id_type=MESH,
+        )
+
+    def cols_own(c):
+        return pltpu.make_async_copy(
+            cols.at[c, me], cols_out.at[rows_at(me * deep, deep), pl.ds(c * picks, picks)],
+            cown.at[c],
+        )
+
+    for c in range(2):
         for k in range(1, freqs):
             rows_copy(c, k).wait_recv()
         rows_own(c).wait()
 
-    def tile(i, carry):
-        at = rows_at(i * 8, 8)
-        for lane in range(0, picks, 128):
-            c, off = lane // half, lane % half
-            points = [
-                (
-                    pick_timed[f, at, lane : lane + 128]
-                    + step * dir_timed[c, f, at, off : off + 128],
-                    pick_timed[f, at, picks + lane : picks + lane + 128]
-                    + step * dir_timed[c, f, at, half + off : half + off + 128],
-                )
-                for f in range(freqs)
-            ]
-            done = shrink_points(points, keep_cols[:, lane : lane + 128], level)
-            for f in range(freqs):
-                cols[f, at, lane : lane + 128] = done[f][0]
-                cols[f, at, picks + lane : picks + lane + 128] = done[f][1]
-        return carry
-
-    lax.fori_loop(0, deep // 8, tile, 0)
-    land = cols_out.at[rows_at(me * deep, deep), :]
-
-    def cols_copy(k):
-        to = (me + k) % freqs
-        return pltpu.make_async_remote_copy(
-            cols.at[to], land, csend.at[k], crecv.at[k],
-            device_id={"freq": to}, device_id_type=MESH,
-        )
-
-    cols_own = pltpu.make_async_copy(cols.at[me], land, cown)
-    for k in range(1, freqs):
-        cols_copy(k).start()
-    cols_own.start()
+        def tile(i, carry):
+            at = rows_at(i * 8, 8)
+            for lane in range(0, half, 128):
+                points = [
+                    (timed[c, f, at, lane : lane + 128],
+                     timed[c, f, at, half + lane : half + lane + 128])
+                    for f in range(freqs)
+                ]
+                good = keep_cols[:, c * half + lane : c * half + lane + 128]
+                done = shrink_points(points, good, level)
+                for f in range(freqs):
+                    cols[c, f, at, lane : lane + 128] = done[f][0]
+                    cols[c, f, at, half + lane : half + lane + 128] = done[f][1]
+            return carry
+
+        lax.fori_loop(0, deep // 8, tile, 0)
+        for k in range(1, freqs):
+            cols_copy(c, k).start()
+        cols_own(c).start()
+    for i in range(lines):
+        for k in range(1, freqs):
+            back_copy(i, k).wait()
+        back_own(i).wait()
+
+    def tail(x_ref, o_ref):
+        x = jnp.concatenate([x_ref[0, 0], x_ref[1, 0]], axis=0)
+        n = x.shape[0]
+        out = lax.dot_general(
+            thirds(x), fill[...], across_lanes, preferred_element_type=jnp.float32
+        )
+        out = (out[:n] + out[n : 2 * n]) + out[2 * n :]
+        o_ref[0, 0] = out[: n // 2]
+        o_ref[1, 0] = out[n // 2 :]
+
+    pltpu.emit_pipeline(
+        tail, grid=(rows // deep,),
+        in_specs=[pl.BlockSpec((2, 1, deep, head), lambda j: (0, 0, j, 0))],
+        out_specs=[pl.BlockSpec((2, 1, deep, picks), lambda j: (0, 0, j, 0))],
+    )(back, tails)
     for group in first + second + sums:
         group.drain()
     for i in range(lines):
         for k in range(1, freqs):
             forth(i, k).wait_send()
-            back_copy(i, k).wait()
-        back_own(i).wait()
     for k in range(1, freqs):
-        spread(k).wait_send()
+        along(k).wait_send()
         for c in range(2):
             rows_copy(c, k).wait_send()
-        cols_copy(k).wait()
-    cols_own.wait()
+            cols_copy(c, k).wait()
+    for c in range(2):
+        cols_own(c).wait()
     for k in range(1, size):
         across(k).wait_send()
 
@@ -684,21 +769,22 @@
     deep = rows // freqs
     lines = deep // LINE
     f32, bf16 = jnp.float32, jnp.bfloat16
-    split = jax.ShapeDtypeStruct((two, freqs, deep, width), f32)
+    split = jax.ShapeDtypeStruct((two, freqs, deep, width - picks), f32)
     vmem = pltpu.VMEM
     return pl.pallas_call(
         functools.partial(main_body, freqs, size),
         out_shape=(
             split,
             split,
-            jax.ShapeDtypeStruct(green.shape, f32),
+            jax.ShapeDtypeStruct((two, 1, rows, width - picks), f32),
+            jax.ShapeDtypeStruct((two, 1, rows, picks), f32),
             jax.ShapeDtypeStruct((rows, two * picks), f32),
             jax.ShapeDtypeStruct((two, 1, rows, picks), f32),
             jax.ShapeDtypeStruct((picks, width), bf16),
             jax.ShapeDtypeStruct((8, width), f32),
         ),
         in_specs=[SMEM, SMEM, VMEM, VMEM, ANY, ANY, ANY],
-        out_specs=(ANY, ANY, ANY, ANY, VMEM, VMEM, VMEM),
+        out_specs=(ANY, ANY, ANY, ANY, ANY, VMEM, VMEM, VMEM),
         scratch_shapes=[
             vmem((two, rows, width), f32),
             vmem((two, 2, rows, width), bf16),
@@ -710,20 +796,21 @@
             vmem((two, rows, picks), f32),
             vmem((rows, picks), f32),
             vmem((width, picks), bf16),
-            vmem((8, width), f32),
+            vmem((picks, width - picks), bf16),
+            vmem((two, freqs * LINE, width - picks), f32),
+            vmem((8, width - picks), f32),
             vmem((8, picks), f32),
-            vmem((freqs, deep, two * picks), f32),
             vmem((2, freqs, deep, picks), f32),
-            vmem((freqs, deep, two * picks), f32),
+            vmem((2, freqs, deep, picks), f32),
             vmem((2, 8, 128), f32),
             vmem((freqs, 2, 8, 128), f32),
             vmem((size, 2, 8, 128), f32),
-            DMA((4,)), DMA(()), DMA(()),
-            DMA((lines, freqs)), DMA((lines, freqs)), DMA(()),
+            DMA((4,)), DMA(()), DMA((2 * (width // picks),)),
+            DMA((lines, freqs)), DMA((lines, freqs)), DMA((lines,)),
             DMA((lines, freqs)), DMA((lines, freqs)), DMA((lines,)),
             DMA((6, 2, size)), DMA((6, 2, size)),
             DMA((2, freqs)), DMA((2, freqs)), DMA((2,)),
-            DMA((freqs,)), DMA((freqs,)), DMA(()),
+            DMA((2, freqs)), DMA((2, freqs)), DMA((2,)),
             DMA((freqs,)), DMA((freqs,)), DMA((size,)), DMA((size,)),
         ],
         compiler_params=pltpu.CompilerParams(
@@ -732,20 +819,30 @@
     )(level, wave, srcs, support, green, data, shots)
 
 
-def join_body(mask_ref, hot_ref, cols_ref, back_ref, resid_ref, o_ref, r_ref):
+def join_body(mask_ref, hot_ref, cols_ref, back_ref, tail_ref, resid_ref, o_ref, r_ref):
     picks = hot_ref.shape[0]
-    hot = hot_ref[...]
+    half = picks // 2
+    rows = cols_ref.shape[0]
     mask = mask_ref[0:1, :] > 0.5
+    both = [
+        jnp.concatenate(
+            [cols_ref[:, at : at + half], cols_ref[:, picks + at : picks + at + half]], axis=1
+        )
+        for at in (0, half)
+    ]
+    wide = spread(jnp.concatenate(both, axis=0), hot_ref[...])
     for part in range(2):
-        spread = select(cols_ref[:, part * picks : (part + 1) * picks], hot)
-        o_ref[part, 0] = jnp.where(mask, spread, back_ref[part, 0])
+        new = wide[part * rows : (part + 1) * rows]
+        head = back_ref.shape[3]
+        o_ref[part, 0, :, :head] = jnp.where(mask[:, :head], new[:, :head], back_ref[part, 0])
+        o_ref[part, 0, :, head:] = jnp.where(mask[:, head:], new[:, head:], tail_ref[part, 0])
     r_ref[...] = resid_ref[...]
 
 
-def join_call(mask, hot, cols, back, resid):
-    two, one, rows, width = back.shape
-    picks = hot.shape[0]
-    tile = rows // 8 if rows % 64 == 0 else rows
+def join_call(mask, hot, cols, back, tails, resid):
+    two, one, rows, head = back.shape
+    picks, width = hot.shape
+    tile = rows // 4 if rows % 32 == 0 else rows
     wide = pl.BlockSpec((two, one, tile, width), lambda i: (0, 0, i, 0))
     thin = pl.BlockSpec((two, one, tile, picks), lambda i: (0, 0, i, 0))
     return pl.pallas_call(
@@ -755,15 +852,16 @@
             pl.BlockSpec((8, width), lambda i: (0, 0)),
             pl.BlockSpec((picks, width), lambda i: (0, 0)),
             pl.BlockSpec((tile, two * picks), lambda i: (i, 0)),
-            wide,
+            pl.BlockSpec((two, one, tile, head), lambda i: (0, 0, i, 0)),
+            thin,
             thin,
         ],
         out_specs=[wide, thin],
         out_shape=[
-            jax.ShapeDtypeStruct(back.shape, jnp.float32),
+            jax.ShapeDtypeStruct((two, one, rows, width), jnp.float32),
             jax.ShapeDtypeStruct(resid.shape, jnp.float32),
         ],
-    )(mask, hot, cols, back, resid)
+    )(mask, hot, cols, back, tails, resid)
 
 
 def pick_body(hot_ref, x_ref, o_ref):
@@ -805,12 +903,13 @@
     size = lax.axis_size("rcv")
     fast = rows_here % (LINE * freqs) == 0 and size > 2 and rows_here // freqs >= 8 * LINE
     fast = fast and rows_here % 32 == 0 and width % picks == 0 and picks % 256 == 0
+    fast = fast and 2 * (width // picks) <= 8 * size - 4
     if fast:
-        _, _, back, cols, resid, hot, mask = main_call(
+        _, _, back, tails, cols, resid, hot, mask = main_call(
             freqs, size, threshold, wavelet[:, 0], sources[None, :], support,
             green_freq, data_matrix, shot_panels,
         )
-        green_next, residual = join_call(mask, hot, cols, back, resid)
+        green_next, residual = join_call(mask, hot, cols, back, tails, resid)
         return (green_next, residual)
     keep_all = support.astype(jnp.float32)
     places = jnp.arange(width, dtype=jnp.int32)

time: 284 us -> 276 us (0.972)
  Pallas kernels: 282 us -> 274 us
    pallas_call x1, Pallas kernels: 268 us -> 262 us  [main_call(): pl.pallas_call(functools.partial(main_body, freqs, size), out_shape=(spli...]
where the time goes in v2:
time: 276 us; the launch traced here: 275 us
  Pallas kernels  274 us (99%)
    pallas_call x1, Pallas kernels, main_call(): pl.pallas_call(functools.partial(main_body, freqs, size), out_shape=(spli...  262 us
    pallas_call x1, Pallas kernels, join_call(): pl.pallas_call(join_body, grid=(rows // tile,), in_specs=[pl.BlockSpec((8...  11.6 us

profile of v2, /device:TPU:1, one launch (start us, length us, event | category | flops | bytes accessed | tf_op | source)
XLA Modules:
  0.0 275.3 jit_solution(15749637653866849383)
XLA Ops:
  1.3 262.4 %shard_map.86 = (f32[2,8,72,2048]{3,2,1,0:T(8,128)}, f32[2,8,72,2048]{3,2,1,0:T(8,128)}, f32[2,1,576,2048]{3,2,1,0:T(8,128)}, f32[2,1,576,256]{3,2,1,0:T(8,128)}...) custom-call(f32[1]{0:T(128)S(6)} %copy.9.level_ref, ...), custom_call_target="tpu_custom_call" | custom-call | tf_op jit(solution)/shard_map/pallas_call | solution.py:774
  263.7 11.6 %shard_map.87 = (f32[2,1,576,2304]{3,2,1,0:T(8,128)}, f32[2,1,576,256]{3,2,1,0:T(8,128)}) custom-call(f32[8,2304]{1,0:T(8,128)} %get-tuple-element.8.mask_ref, bf16[256,2304]{1,0:T(8,128)(2,1)} %get-tuple-element.9.hot_ref, f32[576,512]{1,0:T(8,128)} %get-tuple-element.10.cols_ref, f32[2,1,576,2048]{3,2,1,0:T(8,128)} %get-tuple-element.11.back_ref, ...), custom_call_target="tpu_custom_call" | custom-call | tf_op jit(solution)/shard_map/pallas_call | solution.py:848

commit v3 on v2

--- a/solution.py
+++ b/solution.py
@@ -527,21 +527,23 @@
             grid=(count,), in_specs=[block], out_specs=[block],
         )(gathered, shrunk)
 
+    def back_ends(i, to):
+        line = min(i, lines - 1)
+        part = slice(0, 2) if i < lines - 1 else slice(i - line, i - line + 1)
+        return (
+            shrunk.at[part, to, pl.ds(line * LINE, LINE), :],
+            back.at[part, 0, rows_at(me * deep + line * LINE, LINE), :],
+        )
+
     def back_copy(i, k):
         to = (me + k) % freqs
         return pltpu.make_async_remote_copy(
-            shrunk.at[:, to, pl.ds(i * LINE, LINE), :],
-            back.at[:, 0, rows_at(me * deep + i * LINE, LINE), :],
-            bsend.at[i, k], brecv.at[i, k],
+            *back_ends(i, to), bsend.at[i, k], brecv.at[i, k],
             device_id={"freq": to}, device_id_type=MESH,
         )
 
     def back_own(i):
-        return pltpu.make_async_copy(
-            shrunk.at[:, me, pl.ds(i * LINE, LINE), :],
-            back.at[:, 0, rows_at(me * deep + i * LINE, LINE), :],
-            bown.at[i],
-        )
+        return pltpu.make_async_copy(*back_ends(i, me), bown.at[i])
 
     def give(lo, count):
         for i in range(lo, lo + count):
@@ -614,11 +616,13 @@
     first[1].recv(0)
     first[1].start(1)
     shrink(2, 2)
+    give(0, 4)
     sums[0].recv(0)
     sums[0].start(1)
     first[1].recv(1)
     first[1].start(2)
     shrink(4, 1)
+    give(4, 1)
     sums[0].recv(1)
     sums[0].start(2)
     first[1].recv(2)
@@ -628,31 +632,28 @@
     direction_of(0)
     second[0].start(0)
     shrink(5, 2)
-    give(0, 3)
+    give(5, 2)
     sums[1].recv(0)
     sums[1].start(1)
     second[0].recv(0)
     second[0].start(1)
     shrink(7, 1)
-    give(3, 1)
+    give(7, 1)
     sums[1].recv(1)
     sums[1].start(2)
     second[0].recv(1)
     second[0].start(2)
     shrink(8, lines - 8)
-    give(4, 1)
+    give(8, lines - 8)
     sums[1].recv(2)
     direction_of(1)
     second[1].start(0)
     second[0].recv(2)
     first_norms = image_of(0)
-    give(5, 1)
     second[1].recv(0)
     second[1].start(1)
-    give(6, 1)
     second[1].recv(1)
     second[1].start(2)
-    give(7, lines - 7)
     second[1].recv(2)
     second_norms = image_of(1)
 
@@ -673,6 +674,7 @@
 
     for k in range(1, freqs):
         along(k).start()
+    give(lines, 1)
     parts_sum = norms[...]
     for k in range(1, freqs):
         along(k).wait_recv()
@@ -727,7 +729,7 @@
         for k in range(1, freqs):
             cols_copy(c, k).start()
         cols_own(c).start()
-    for i in range(lines):
+    for i in range(lines + 1):
         for k in range(1, freqs):
             back_copy(i, k).wait()
         back_own(i).wait()
@@ -807,7 +809,7 @@
             vmem((size, 2, 8, 128), f32),
             DMA((4,)), DMA(()), DMA((2 * (width // picks),)),
             DMA((lines, freqs)), DMA((lines, freqs)), DMA((lines,)),
-            DMA((lines, freqs)), DMA((lines, freqs)), DMA((lines,)),
+            DMA((lines + 1, freqs)), DMA((lines + 1, freqs)), DMA((lines + 1,)),
             DMA((6, 2, size)), DMA((6, 2, size)),
             DMA((2, freqs)), DMA((2, freqs)), DMA((2,)),
             DMA((2, freqs)), DMA((2, freqs)), DMA((2,)),
@@ -819,18 +821,29 @@
     )(level, wave, srcs, support, green, data, shots)
 
 
-def join_body(mask_ref, hot_ref, cols_ref, back_ref, tail_ref, resid_ref, o_ref, r_ref):
+def join_body(mask_ref, hot_ref, cols_ref, back_ref, tail_ref, resid_ref, o_ref, r_ref, stacked):
     picks = hot_ref.shape[0]
     half = picks // 2
     rows = cols_ref.shape[0]
     mask = mask_ref[0:1, :] > 0.5
+
+    @pl.when(pl.program_id(0) == 0)
+    def _():
+        for n in range(3):
+            stacked[n * picks : (n + 1) * picks, :] = hot_ref[...]
+
     both = [
         jnp.concatenate(
             [cols_ref[:, at : at + half], cols_ref[:, picks + at : picks + at + half]], axis=1
         )
         for at in (0, half)
     ]
-    wide = spread(jnp.concatenate(both, axis=0), hot_ref[...])
+    x = jnp.concatenate(both, axis=0)
+    hi, mid = halves(x)
+    low = (x - hi.astype(jnp.float32) - mid.astype(jnp.float32)).astype(jnp.bfloat16)
+    wide = jnp.dot(
+        jnp.concatenate([hi, mid, low], axis=1), stacked[...], preferred_element_type=jnp.float32
+    )
     for part in range(2):
         new = wide[part * rows : (part + 1) * rows]
         head = back_ref.shape[3]
@@ -861,6 +874,7 @@
             jax.ShapeDtypeStruct((two, one, rows, width), jnp.float32),
             jax.ShapeDtypeStruct(resid.shape, jnp.float32),
         ],
+        scratch_shapes=[pltpu.VMEM((3 * picks, width), jnp.bfloat16)],
     )(mask, hot, cols, back, tails, resid)
 
 
@@ -901,7 +915,7 @@
     picks = sources.shape[0]
     freqs = lax.axis_size("freq")
     size = lax.axis_size("rcv")
-    fast = rows_here % (LINE * freqs) == 0 and size > 2 and rows_here // freqs >= 8 * LINE
+    fast = rows_here % (LINE * freqs) == 0 and size > 2 and rows_here // freqs >= 9 * LINE
     fast = fast and rows_here % 32 == 0 and width % picks == 0 and picks % 256 == 0
     fast = fast and 2 * (width // picks) <= 8 * size - 4
     if fast:

time: 276 us -> 272 us (0.986)
  Pallas kernels: 274 us -> 270 us
    pallas_call x1, Pallas kernels: 262 us -> 258 us  [main_call(): pl.pallas_call(functools.partial(main_body, freqs, size), out_shape=(spli...]
where the time goes in v3:
time: 272 us; the launch traced here: 271 us
  Pallas kernels  270 us (99%)
    pallas_call x1, Pallas kernels, main_call(): pl.pallas_call(functools.partial(main_body, freqs, size), out_shape=(spli...  258 us
    pallas_call x1, Pallas kernels, join_call(): pl.pallas_call(join_body, grid=(rows // tile,), in_specs=[pl.BlockSpec((8...  11.8 us

profile of v3, /device:TPU:1, one launch (start us, length us, event | category | flops | bytes accessed | tf_op | source)
XLA Modules:
  0.0 271.4 jit_solution(11610396587254518340)
XLA Ops:
  1.3 258.3 %shard_map.86 = (f32[2,8,72,2048]{3,2,1,0:T(8,128)}, f32[2,8,72,2048]{3,2,1,0:T(8,128)}, f32[2,1,576,2048]{3,2,1,0:T(8,128)}, f32[2,1,576,256]{3,2,1,0:T(8,128)}...) custom-call(f32[1]{0:T(128)S(6)} %copy.9.level_ref, ...), custom_call_target="tpu_custom_call" | custom-call | tf_op jit(solution)/shard_map/pallas_call | solution.py:776
  259.6 11.8 %shard_map.87 = (f32[2,1,576,2304]{3,2,1,0:T(8,128)}, f32[2,1,576,256]{3,2,1,0:T(8,128)}) custom-call(f32[8,2304]{1,0:T(8,128)} %get-tuple-element.8.mask_ref, bf16[256,2304]{1,0:T(8,128)(2,1)} %get-tuple-element.9.hot_ref, f32[576,512]{1,0:T(8,128)} %get-tuple-element.10.cols_ref, f32[2,1,576,2048]{3,2,1,0:T(8,128)} %get-tuple-element.11.back_ref, ...), custom_call_target="tpu_custom_call" | custom-call | tf_op jit(solution)/shard_map/pallas_call | solution.py:861

commit v4 on v3

--- a/solution.py
+++ b/solution.py
@@ -359,10 +359,11 @@
 
 def main_body(
     freqs, size, level_ref, wave, srcs, support, green, data_hbm, shots_hbm,
-    gathered, shrunk, back, tails, cols_out, residual, hot_out, mask_out,
+    gathered, shrunk, back, tails, cols_out, resid_hbm, hot_hbm, mask_hbm,
+    residual, hot_out, mask_out,
     big, data, whole, dir_all, adjoint, held, local, shots, image, hot, fill, lead,
     keep, keep_cols, timed, cols, norms, freq_box, rcv_box,
-    gload, sload, load, fsend, frecv, fown, bsend, brecv, bown,
+    gload, sload, load, put, fsend, frecv, fown, bsend, brecv, bown,
     zsend, zrecv, dsend, drecv, down, csend, crecv, cown, nfs, nfr, nzs, nzr,
 ):
     me = lax.axis_index("freq")
@@ -628,6 +629,14 @@
     first[1].recv(2)
     residual_of(1)
     sums[1].start(0)
+    puts = [
+        pltpu.make_async_copy(src, dst, put.at[n])
+        for n, (src, dst) in enumerate(
+            ((residual, resid_hbm), (hot_out, hot_hbm), (mask_out, mask_hbm))
+        )
+    ]
+    for copy in puts:
+        copy.start()
     sums[0].recv(2)
     direction_of(0)
     second[0].start(0)
@@ -662,30 +671,30 @@
 
     def along(k):
         return pltpu.make_async_remote_copy(
-            norms, freq_box.at[k], nfs.at[k], nfr.at[k],
+            freq_box.at[0], freq_box.at[k], nfs.at[k], nfr.at[k],
             device_id={"freq": (me + k) % freqs}, device_id_type=MESH,
         )
 
     def across(k):
         return pltpu.make_async_remote_copy(
-            rcv_box.at[0], rcv_box.at[k], nzs.at[k], nzr.at[k],
+            norms, rcv_box.at[k], nzs.at[k], nzr.at[k],
             device_id={"rcv": (z + k) % size}, device_id_type=MESH,
         )
 
+    for k in range(1, size):
+        across(k).start()
+    line_sum = norms[...]
+    for k in range(1, size):
+        across(k).wait_recv()
+        line_sum = line_sum + rcv_box[k]
+    freq_box[0] = line_sum
     for k in range(1, freqs):
         along(k).start()
     give(lines, 1)
-    parts_sum = norms[...]
+    total = line_sum
     for k in range(1, freqs):
         along(k).wait_recv()
-        parts_sum = parts_sum + freq_box[k]
-    rcv_box[0] = parts_sum
-    for k in range(1, size):
-        across(k).start()
-    total = parts_sum
-    for k in range(1, size):
-        across(k).wait_recv()
-        total = total + rcv_box[k]
+        total = total + freq_box[k]
     step = total[0] / total[1]
     level = level_ref[0]
     for c in range(2):
@@ -749,6 +758,8 @@
         in_specs=[pl.BlockSpec((2, 1, deep, head), lambda j: (0, 0, j, 0))],
         out_specs=[pl.BlockSpec((2, 1, deep, picks), lambda j: (0, 0, j, 0))],
     )(back, tails)
+    for copy in puts:
+        copy.wait()
     for group in first + second + sums:
         group.drain()
     for i in range(lines):
@@ -786,8 +797,11 @@
             jax.ShapeDtypeStruct((8, width), f32),
         ),
         in_specs=[SMEM, SMEM, VMEM, VMEM, ANY, ANY, ANY],
-        out_specs=(ANY, ANY, ANY, ANY, ANY, VMEM, VMEM, VMEM),
+        out_specs=(ANY,) * 8,
         scratch_shapes=[
+            vmem((two, 1, rows, picks), f32),
+            vmem((picks, width), bf16),
+            vmem((8, width), f32),
             vmem((two, rows, width), f32),
             vmem((two, 2, rows, width), bf16),
             vmem((2, size * rows, picks), f32),
@@ -807,7 +821,7 @@
             vmem((2, 8, 128), f32),
             vmem((freqs, 2, 8, 128), f32),
             vmem((size, 2, 8, 128), f32),
-            DMA((4,)), DMA(()), DMA((2 * (width // picks),)),
+            DMA((4,)), DMA(()), DMA((2 * (width // picks),)), DMA((3,)),
             DMA((lines, freqs)), DMA((lines, freqs)), DMA((lines,)),
             DMA((lines + 1, freqs)), DMA((lines + 1, freqs)), DMA((lines + 1,)),
             DMA((6, 2, size)), DMA((6, 2, size)),
@@ -855,7 +869,7 @@
 def join_call(mask, hot, cols, back, tails, resid):
     two, one, rows, head = back.shape
     picks, width = hot.shape
-    tile = rows // 4 if rows % 32 == 0 else rows
+    tile = rows // 6 if rows % 48 == 0 else rows
     wide = pl.BlockSpec((two, one, tile, width), lambda i: (0, 0, i, 0))
     thin = pl.BlockSpec((two, one, tile, picks), lambda i: (0, 0, i, 0))
     return pl.pallas_call(

time: 272 us -> 275 us (1.011)
  Pallas kernels: 270 us -> 273 us
where the time goes in v4:
time: 275 us; the launch traced here: 274 us
  Pallas kernels  273 us (99%)
    pallas_call x1, Pallas kernels, main_call(): pl.pallas_call(functools.partial(main_body, freqs, size), out_shape=(spli...  260 us
    pallas_call x1, Pallas kernels, join_call(): pl.pallas_call(join_body, grid=(rows // tile,), in_specs=[pl.BlockSpec((8...  13 us

profile of v4, /device:TPU:1, one launch (start us, length us, event | category | flops | bytes accessed | tf_op | source)
XLA Modules:
  0.0 274.3 jit_solution(7436794253340728489)
XLA Ops:
  1.3 260.0 %shard_map.86 = (f32[2,8,72,2048]{3,2,1,0:T(8,128)}, f32[2,8,72,2048]{3,2,1,0:T(8,128)}, f32[2,1,576,2048]{3,2,1,0:T(8,128)}, f32[2,1,576,256]{3,2,1,0:T(8,128)}...) custom-call(f32[1]{0:T(128)S(6)} %copy.9.level_ref, ...), custom_call_target="tpu_custom_call" | custom-call | tf_op jit(solution)/shard_map/pallas_call | solution.py:787
  261.3 13.0 %shard_map.87 = (f32[2,1,576,2304]{3,2,1,0:T(8,128)}, f32[2,1,576,256]{3,2,1,0:T(8,128)}) custom-call(f32[8,2304]{1,0:T(8,128)} %get-tuple-element.8.mask_ref, bf16[256,2304]{1,0:T(8,128)(2,1)} %get-tuple-element.9.hot_ref, f32[576,512]{1,0:T(8,128)} %get-tuple-element.10.cols_ref, f32[2,1,576,2048]{3,2,1,0:T(8,128)} %get-tuple-element.11.back_ref, ...), custom_call_target="tpu_custom_call" | custom-call | tf_op jit(solution)/shard_map/pallas_call | solution.py:875
